TPU v7x, 256 devices: a whole 4x4x8 slice. The times are simulated.
256 devices in a mesh: stn: 16 (over x, y_lo, core), chan: 16 (over z, y_hi).
Axes of the slice: x: 4, y: 4 (y_hi: 2, y_lo: 2; y = y_hi * 2 + y_lo), z: 8, core: 2. Of those that a mesh axis runs over, the one named last changes fastest.
Arguments:
- volts: bfloat16 [16, 2, 1024, 18048], P('chan', None, 'stn'), may hold values from -6 to 6
- taps: float32 [16, 384], replicated, may hold values from -1.5 to 1.5
- survive: int32 [16, 8], replicated, may hold values from 0 to 383, as said below
- owner: int32 [16, 8], replicated, may hold values from 0 to 15, as said below
Outputs:
- visibilities: bfloat16 [16, 24, 2, 1024, 1024], P('chan', None, None, 'stn')
Inputs may be any that keep to these rules, and one draw needn't show every extreme that they name: `survive`: each band lists 8 distinct fine channels. Within one band at most 2 channels share an owner, and in some band exactly 2 do; each owner holds at most 24 channels in all, and one owner holds exactly 24.
All inputs are finite; a program needn't handle non-finite values.
Results may differ from a plain program's by a relative error of at most 0.0076.
Values may be sent and summed in bfloat16 or wider, within the bound.
A program may use at most 128 MiB of HBM per device.

v0:
```python
import math

import jax
import jax.numpy as jnp
from jax import lax
from jax.sharding import PartitionSpec as P

RCAP = 24


def shifted(x, axis, by):
    peers = lax.axis_size(axis)
    return lax.ppermute(x, axis, [(i, (i + by) % peers) for i in range(peers)])


def fine_tables(chosen, fine_len):
    branch_ids = jnp.arange(fine_len, dtype=jnp.int32)
    phase_index = chosen[:, None] * branch_ids[None, :] % fine_len
    angles = phase_index.astype(jnp.float32) * (2.0 * math.pi / fine_len)
    factor = 1.0 / math.sqrt(fine_len)
    cosine = (jnp.cos(angles) * factor).astype(jnp.bfloat16)
    sine_table = (jnp.sin(angles) * factor).astype(jnp.bfloat16)
    return (cosine, sine_table)


def polyphase(signal, taps, spectra_count):
    accum = jnp.zeros((2, signal.shape[1], spectra_count, signal.shape[3]), jnp.float32)
    for tap_index in range(taps.shape[0]):
        accum = accum + taps[tap_index] * signal[
            :, :, tap_index : tap_index + spectra_count, :
        ].astype(jnp.float32)
    return accum.astype(jnp.bfloat16)


def split_parts(products, inputs, spectra_count):
    real_part = products[..., :inputs, :inputs] + products[..., inputs:, inputs:]
    imag_part = products[..., inputs:, :inputs] - products[..., :inputs, inputs:]
    return (jnp.stack([real_part, imag_part], axis=-3) / spectra_count).astype(jnp.bfloat16)


def per_device(volts, taps, survive, owner):
    band_index = lax.axis_index("chan")
    chan_count = lax.axis_size("chan")
    stn_count = lax.axis_size("stn")
    stn_index = lax.axis_index("stn")
    inputs = volts.shape[2]
    samples = volts.shape[3]
    taps_count, fine_len = taps.shape
    keep_count = survive.shape[1]
    spectra_count = samples // fine_len - taps_count + 1
    slot_cap = max(2, (RCAP + chan_count - 1) // chan_count)
    chosen = lax.dynamic_index_in_dim(survive, band_index, 0, keepdims=False)
    signal = volts[0].reshape(2, inputs, samples // fine_len, fine_len)
    filtered = polyphase(signal, taps, spectra_count)
    signal_rows = filtered.transpose(1, 2, 0, 3).reshape(inputs * spectra_count, 2 * fine_len)
    cosine, sine_table = fine_tables(chosen, fine_len)
    dft_table = jnp.concatenate(
        [
            jnp.concatenate([cosine.T, -sine_table.T], 1),
            jnp.concatenate([sine_table.T, cosine.T], 1),
        ],
        0,
    )
    spectra = jnp.dot(signal_rows, dft_table, preferred_element_type=jnp.float32).astype(
        jnp.bfloat16
    )
    spectra = spectra.reshape(inputs, spectra_count, 2, keep_count).transpose(3, 1, 2, 0)
    spectra = spectra.reshape(keep_count, spectra_count * 2 * inputs)
    owner_ids = jnp.arange(chan_count, dtype=jnp.int32)
    owner_hits = (owner[:, :, None] == owner_ids).astype(jnp.int32)
    pair_rank = jnp.sum((jnp.cumsum(owner_hits, 1) - owner_hits) * owner_hits, 2)
    flat_hits = owner_hits.reshape(-1, chan_count)
    owner_slot = jnp.sum((jnp.cumsum(flat_hits, 0) - flat_hits) * flat_hits, 1)
    my_target = lax.dynamic_index_in_dim(
        owner * slot_cap + pair_rank, band_index, 0, keepdims=False
    )
    send_slots = jnp.arange(chan_count * slot_cap, dtype=jnp.int32)
    send_pick = (send_slots[:, None] == my_target[None, :]).astype(jnp.bfloat16)
    outgoing = jnp.dot(send_pick, spectra, preferred_element_type=jnp.float32).astype(jnp.bfloat16)
    outgoing = outgoing.reshape(chan_count, slot_cap, spectra_count, 2 * inputs)
    arrived = lax.all_to_all(outgoing, "chan", split_axis=0, concat_axis=0, tiled=True)
    source_ids = jnp.arange(owner.shape[0], dtype=jnp.int32)
    slot_column = (source_ids[:, None] * slot_cap + pair_rank).reshape(-1)
    is_mine = (owner == band_index).reshape(-1)
    slot_rows = (
        (jnp.arange(RCAP, dtype=jnp.int32)[:, None] == owner_slot[None, :]) & is_mine[None, :]
    ).astype(jnp.bfloat16)
    slot_cols = (slot_column[:, None] == send_slots[None, :]).astype(jnp.bfloat16)
    compact_map = jnp.dot(slot_rows, slot_cols, preferred_element_type=jnp.float32).astype(
        jnp.bfloat16
    )
    local_block = jnp.dot(
        compact_map, arrived.reshape(chan_count * slot_cap, -1), preferred_element_type=jnp.float32
    ).astype(jnp.bfloat16)
    local_block = local_block.reshape(RCAP, spectra_count, 2 * inputs)

    def place(totals, remote_block, anchor):
        products = jnp.einsum(
            "stp,stq->spq", local_block, remote_block, preferred_element_type=jnp.float32
        )
        return lax.dynamic_update_slice_in_dim(
            totals, split_parts(products, inputs, spectra_count)[None], anchor, 0
        )

    empty_out = jnp.zeros((stn_count, RCAP, 2, inputs, inputs), jnp.bfloat16)
    totals = place(empty_out, local_block, stn_index)

    def one_step(turn_index, carry):
        remote_block, partial_out = carry
        remote_block = shifted(remote_block, "stn", 1)
        partial_out = place(partial_out, remote_block, (stn_index - turn_index) % stn_count)
        return (remote_block, partial_out)

    remote_block, totals = lax.fori_loop(1, stn_count, one_step, (local_block, totals))
    visibilities = totals.transpose(1, 2, 3, 0, 4).reshape(RCAP, 2, inputs, stn_count * inputs)
    return visibilities[None]


def solution(mesh):
    return jax.shard_map(
        per_device,
        mesh=mesh,
        in_specs=(P("chan", None, "stn", None), P(), P(), P()),
        out_specs=P("chan", None, None, "stn", None),
        check_vma=False,
    )
```

profile of v0, /device:TPU:1, one launch (start us, length us, event | category | flops | bytes accessed | tf_op | source)
XLA Modules:
  0.0 253.4 jit_solution(10427993000819978665)
XLA Ops:
  0.0 0.7 copy-done
  1.2 0.8 copy.24
  1.9 1.1 slice_reduce_fusion.15
  3.6 7.8 %reshape_squeeze.3 = bf16[2,64,47,384]{3,2,1,0:T(8,128)(2,1)} reshape(bf16[1,2,64,18048]{3,2,1,0:T(8,128)(2,1)} %param.6) | data formatting | bytes 9240576 | tf_op jit(solution)/shard_map/reshape;squeeze | solution.py:53
  11.5 32.6 %fusion.4 = bf16[64,32,2,384]{3,1,0,2:T(8,128)(2,1)S(1)} fusion(bf16[2,64,47,384]{3,2,1,0:T(8,128)(2,1)} %reshape_squeeze.3, f32[384]{0:T(512)S(1)} %get-tuple-element.153, f32[384]{0:T(512)S(1)} %get-tuple-element.154, f32[384]{0:T(512)S(1)} %get-tuple-element.140, f32[384]{0:T(512)S(1)} %get-tuple-element.141, f32[384]{0:T(512)S(1)} %get-tuple-element.142, ...), kind=kLoop, calls=%fused_computation.10 | loop fusion | flops 75497472 | bytes 53501952 | tf_op jit(solution)/shard_map/transpose | solution.py:55
  44.1 3.2 %copy.28 = bf16[64,32,2,384]{3,2,1,0:T(2,128)(2,1)S(1)} copy(bf16[64,32,2,384]{3,1,0,2:T(8,128)(2,1)S(1)} %fusion.4) | data formatting | bytes 6291456 | tf_op jit(solution)/shard_map/transpose | solution.py:55
  48.0 0.9 convolution_convert_fusion.2
  49.7 0.7 copy.32
  50.4 11.8 %all-to-all-start = ((bf16[16,2,32,128]{3,2,1,0:T(8,128)(2,1)}), bf16[16,2,32,128]{3,2,1,0:T(8,128)(2,1)S(1)}, u32[]{:S(2)}, u32[]{:S(2)}) async-start(bf16[16,2,32,128]{3,2,1,0:T(8,128)(2,1)} %bitcast.15), calls=%async_computation | async-start | bytes 524288 | tf_op jit(solution)/shard_map/all_to_all | solution.py:81
  63.1 11.1 %all-to-all-done = bf16[16,2,32,128]{3,2,1,0:T(8,128)(2,1)S(1)} async-done(((bf16[16,2,32,128]{3,2,1,0:T(8,128)(2,1)}), bf16[16,2,32,128]{3,2,1,0:T(8,128)(2,1)S(1)}, u32[]{:S(2)}, u32[]{:S(2)}) %all-to-all-start) | async-done | bytes 262176 | tf_op jit(solution)/shard_map/all_to_all | solution.py:81
  75.5 7.8 %broadcast_in_dim.4 = bf16[16,24,2,64,64]{4,3,1,2,0:T(8,128)(2,1)} broadcast(bf16[]{:T(256)} %constant.103.clone.1), dimensions={} | broadcast | bytes 6291458 | tf_op jit(solution)/shard_map/broadcast_in_dim | solution.py:105
  83.3 1.2 fusion.8
  84.5 136.5 %while.17 = (s32[]{:T(128)}, bf16[24,32,128]{2,1,0:T(8,128)(2,1)S(1)}, bf16[16,24,2,64,64]{4,3,1,2,0:T(8,128)(2,1)}, bf16[24,32,128]{2,1,0:T(8,128)(2,1)S(1)}, s...) while((s32[]{:T(128)}, bf16[24,32,128]{2,1,0:T(8,128)(2,1)S(1)}, ...), condition=%wide.region_5.6_spmd, body=%wide.region_4.5_spmd.sunk | while | flops 25952272 | bytes 7078180 | solution.py:114
  84.5 2.8 %collective-permute-start = (bf16[24,32,128]{2,1,0:T(8,128)(2,1)S(1)}, bf16[24,32,128]{2,1,0:T(8,128)(2,1)S(1)}, u32[]{:S(2)}, u32[]{:S(2)}) collective-permute-start(bf16[24,32,128]{2,1,0:T(8,128)(2,1)S(1)} %get-tuple-element.216), channel_id=1, source_target_pairs={{0,16},{16,32},{32,48},{48,64},{64,80},{80,96},{96,112},{112,128},... | collective-permute-start | bytes 589832 | tf_op jit(solution)/shard_map/while/body/eval_jaxpr/ppermute | solution.py:13
  87.3 2.6 %collective-permute-done = bf16[24,32,128]{2,1,0:T(8,128)(2,1)S(1)} collective-permute-done((bf16[24,32,128]{2,1,0:T(8,128)(2,1)S(1)}, bf16[24,32,128]{2,1,0:T(8,128)(2,1)S(1)}, u32[]{:S(2)}, u32[]{:S(2)}) %collective-permute-start) | collective-permute-done | bytes 196640 | tf_op jit(solution)/shard_map/while/body/eval_jaxpr/ppermute | solution.py:13
  90.8 1.1 fusion.59
  91.9 2.6 %collective-permute-start = (bf16[24,32,128]{2,1,0:T(8,128)(2,1)S(1)}, bf16[24,32,128]{2,1,0:T(8,128)(2,1)S(1)}, u32[]{:S(2)}, u32[]{:S(2)}) collective-permute-start(bf16[24,32,128]{2,1,0:T(8,128)(2,1)S(1)} %get-tuple-element.216), channel_id=1, source_target_pairs={{0,16},{16,32},{32,48},{48,64},{64,80},{80,96},{96,112},{112,128},... | collective-permute-start | bytes 589832 | tf_op jit(solution)/shard_map/while/body/eval_jaxpr/ppermute | solution.py:13
  94.5 2.7 %collective-permute-done = bf16[24,32,128]{2,1,0:T(8,128)(2,1)S(1)} collective-permute-done((bf16[24,32,128]{2,1,0:T(8,128)(2,1)S(1)}, bf16[24,32,128]{2,1,0:T(8,128)(2,1)S(1)}, u32[]{:S(2)}, u32[]{:S(2)}) %collective-permute-start) | collective-permute-done | bytes 196640 | tf_op jit(solution)/shard_map/while/body/eval_jaxpr/ppermute | solution.py:13
  98.2 1.1 fusion.59
  99.3 2.4 collective-permute-start
  101.7 4.9 %collective-permute-done = bf16[24,32,128]{2,1,0:T(8,128)(2,1)S(1)} collective-permute-done((bf16[24,32,128]{2,1,0:T(8,128)(2,1)S(1)}, bf16[24,32,128]{2,1,0:T(8,128)(2,1)S(1)}, u32[]{:S(2)}, u32[]{:S(2)}) %collective-permute-start) | collective-permute-done | bytes 196640 | tf_op jit(solution)/shard_map/while/body/eval_jaxpr/ppermute | solution.py:13
  107.5 1.2 fusion.59
  109.0 7.0 %collective-permute-done = bf16[24,32,128]{2,1,0:T(8,128)(2,1)S(1)} collective-permute-done((bf16[24,32,128]{2,1,0:T(8,128)(2,1)S(1)}, bf16[24,32,128]{2,1,0:T(8,128)(2,1)S(1)}, u32[]{:S(2)}, u32[]{:S(2)}) %collective-permute-start) | collective-permute-done | bytes 196640 | tf_op jit(solution)/shard_map/while/body/eval_jaxpr/ppermute | solution.py:13
  116.9 1.2 fusion.59
  118.2 7.1 %collective-permute-done = bf16[24,32,128]{2,1,0:T(8,128)(2,1)S(1)} collective-permute-done((bf16[24,32,128]{2,1,0:T(8,128)(2,1)S(1)}, bf16[24,32,128]{2,1,0:T(8,128)(2,1)S(1)}, u32[]{:S(2)}, u32[]{:S(2)}) %collective-permute-start) | collective-permute-done | bytes 196640 | tf_op jit(solution)/shard_map/while/body/eval_jaxpr/ppermute | solution.py:13
  126.2 1.1 fusion.59
  127.5 7.3 %collective-permute-done = bf16[24,32,128]{2,1,0:T(8,128)(2,1)S(1)} collective-permute-done((bf16[24,32,128]{2,1,0:T(8,128)(2,1)S(1)}, bf16[24,32,128]{2,1,0:T(8,128)(2,1)S(1)}, u32[]{:S(2)}, u32[]{:S(2)}) %collective-permute-start) | collective-permute-done | bytes 196640 | tf_op jit(solution)/shard_map/while/body/eval_jaxpr/ppermute | solution.py:13
  135.7 1.2 fusion.59
  137.0 7.1 %collective-permute-done = bf16[24,32,128]{2,1,0:T(8,128)(2,1)S(1)} collective-permute-done((bf16[24,32,128]{2,1,0:T(8,128)(2,1)S(1)}, bf16[24,32,128]{2,1,0:T(8,128)(2,1)S(1)}, u32[]{:S(2)}, u32[]{:S(2)}) %collective-permute-start) | collective-permute-done | bytes 196640 | tf_op jit(solution)/shard_map/while/body/eval_jaxpr/ppermute | solution.py:13
  145.1 1.2 fusion.59
  146.4 7.1 %collective-permute-done = bf16[24,32,128]{2,1,0:T(8,128)(2,1)S(1)} collective-permute-done((bf16[24,32,128]{2,1,0:T(8,128)(2,1)S(1)}, bf16[24,32,128]{2,1,0:T(8,128)(2,1)S(1)}, u32[]{:S(2)}, u32[]{:S(2)}) %collective-permute-start) | collective-permute-done | bytes 196640 | tf_op jit(solution)/shard_map/while/body/eval_jaxpr/ppermute | solution.py:13
  154.4 1.1 fusion.59
  155.7 7.2 %collective-permute-done = bf16[24,32,128]{2,1,0:T(8,128)(2,1)S(1)} collective-permute-done((bf16[24,32,128]{2,1,0:T(8,128)(2,1)S(1)}, bf16[24,32,128]{2,1,0:T(8,128)(2,1)S(1)}, u32[]{:S(2)}, u32[]{:S(2)}) %collective-permute-start) | collective-permute-done | bytes 196640 | tf_op jit(solution)/shard_map/while/body/eval_jaxpr/ppermute | solution.py:13
  163.7 1.1 fusion.59
  165.0 7.2 %collective-permute-done = bf16[24,32,128]{2,1,0:T(8,128)(2,1)S(1)} collective-permute-done((bf16[24,32,128]{2,1,0:T(8,128)(2,1)S(1)}, bf16[24,32,128]{2,1,0:T(8,128)(2,1)S(1)}, u32[]{:S(2)}, u32[]{:S(2)}) %collective-permute-start) | collective-permute-done | bytes 196640 | tf_op jit(solution)/shard_map/while/body/eval_jaxpr/ppermute | solution.py:13
  173.1 1.2 fusion.59
  174.5 7.1 %collective-permute-done = bf16[24,32,128]{2,1,0:T(8,128)(2,1)S(1)} collective-permute-done((bf16[24,32,128]{2,1,0:T(8,128)(2,1)S(1)}, bf16[24,32,128]{2,1,0:T(8,128)(2,1)S(1)}, u32[]{:S(2)}, u32[]{:S(2)}) %collective-permute-start) | collective-permute-done | bytes 196640 | tf_op jit(solution)/shard_map/while/body/eval_jaxpr/ppermute | solution.py:13
  182.5 1.1 fusion.59
  183.8 7.2 %collective-permute-done = bf16[24,32,128]{2,1,0:T(8,128)(2,1)S(1)} collective-permute-done((bf16[24,32,128]{2,1,0:T(8,128)(2,1)S(1)}, bf16[24,32,128]{2,1,0:T(8,128)(2,1)S(1)}, u32[]{:S(2)}, u32[]{:S(2)}) %collective-permute-start) | collective-permute-done | bytes 196640 | tf_op jit(solution)/shard_map/while/body/eval_jaxpr/ppermute | solution.py:13
  191.8 1.1 fusion.59
  193.1 7.2 %collective-permute-done = bf16[24,32,128]{2,1,0:T(8,128)(2,1)S(1)} collective-permute-done((bf16[24,32,128]{2,1,0:T(8,128)(2,1)S(1)}, bf16[24,32,128]{2,1,0:T(8,128)(2,1)S(1)}, u32[]{:S(2)}, u32[]{:S(2)}) %collective-permute-start) | collective-permute-done | bytes 196640 | tf_op jit(solution)/shard_map/while/body/eval_jaxpr/ppermute | solution.py:13
  201.2 1.1 fusion.59
  202.4 7.2 %collective-permute-done = bf16[24,32,128]{2,1,0:T(8,128)(2,1)S(1)} collective-permute-done((bf16[24,32,128]{2,1,0:T(8,128)(2,1)S(1)}, bf16[24,32,128]{2,1,0:T(8,128)(2,1)S(1)}, u32[]{:S(2)}, u32[]{:S(2)}) %collective-permute-start) | collective-permute-done | bytes 196640 | tf_op jit(solution)/shard_map/while/body/eval_jaxpr/ppermute | solution.py:13
  210.5 1.1 fusion.59
  211.8 7.2 %collective-permute-done = bf16[24,32,128]{2,1,0:T(8,128)(2,1)S(1)} collective-permute-done((bf16[24,32,128]{2,1,0:T(8,128)(2,1)S(1)}, bf16[24,32,128]{2,1,0:T(8,128)(2,1)S(1)}, u32[]{:S(2)}, u32[]{:S(2)}) %collective-permute-start) | collective-permute-done | bytes 196640 | tf_op jit(solution)/shard_map/while/body/eval_jaxpr/ppermute | solution.py:13
  219.9 1.1 fusion.59
  221.0 15.1 %copy.30 = bf16[24,2,64,16,64]{4,3,2,1,0:T(8,128)(2,1)} copy(bf16[24,2,64,16,64]{4,2,0,1,3:T(8,128)(2,1)} %bitcast.47) | data formatting | bytes 12582912 | tf_op jit(solution)/shard_map/transpose | solution.py:115
  236.2 17.2 %broadcast_in_dim_reshape.2 = bf16[1,24,2,64,1024]{4,3,2,1,0:T(8,128)(2,1)} reshape(bf16[24,2,64,16,64]{4,3,2,1,0:T(8,128)(2,1)} %copy.30) | data formatting | bytes 12582912 | tf_op jit(solution)/shard_map/broadcast_in_dim;reshape | solution.py:116
  (87 shorter events, 19.4 us)
Async XLA Ops:
  0.0 0.7 copy-start
  47.3 15.0 %copy-start.1 = (s32[16,8]{0,1:T(8,128)S(1)}, s32[16,8]{0,1:T(8,128)}, u32[]{:S(2)}) copy-start(s32[16,8]{0,1:T(8,128)} %param.9) | copy-start | bytes 1540
  50.4 23.8 %all-to-all-start = ((bf16[16,2,32,128]{3,2,1,0:T(8,128)(2,1)}), bf16[16,2,32,128]{3,2,1,0:T(8,128)(2,1)S(1)}, u32[]{:S(2)}, u32[]{:S(2)}) async-start(bf16[16,2,32,128]{3,2,1,0:T(8,128)(2,1)} %bitcast.15), calls=%async_computation | async-start | bytes 524288 | tf_op jit(solution)/shard_map/all_to_all | solution.py:81
  84.5 5.4 %collective-permute-start = (bf16[24,32,128]{2,1,0:T(8,128)(2,1)S(1)}, bf16[24,32,128]{2,1,0:T(8,128)(2,1)S(1)}, u32[]{:S(2)}, u32[]{:S(2)}) collective-permute-start(bf16[24,32,128]{2,1,0:T(8,128)(2,1)S(1)} %get-tuple-element.216), channel_id=1, source_target_pairs={{0,16},{16,32},{32,48},{48,64},{64,80},{80,96},{96,112},{112,128},... | collective-permute-start | bytes 589832 | tf_op jit(solution)/shard_map/while/body/eval_jaxpr/ppermute | solution.py:13
  91.9 5.3 %collective-permute-start = (bf16[24,32,128]{2,1,0:T(8,128)(2,1)S(1)}, bf16[24,32,128]{2,1,0:T(8,128)(2,1)S(1)}, u32[]{:S(2)}, u32[]{:S(2)}) collective-permute-start(bf16[24,32,128]{2,1,0:T(8,128)(2,1)S(1)} %get-tuple-element.216), channel_id=1, source_target_pairs={{0,16},{16,32},{32,48},{48,64},{64,80},{80,96},{96,112},{112,128},... | collective-permute-start | bytes 589832 | tf_op jit(solution)/shard_map/while/body/eval_jaxpr/ppermute | solution.py:13
  99.3 7.3 %collective-permute-start = (bf16[24,32,128]{2,1,0:T(8,128)(2,1)S(1)}, bf16[24,32,128]{2,1,0:T(8,128)(2,1)S(1)}, u32[]{:S(2)}, u32[]{:S(2)}) collective-permute-start(bf16[24,32,128]{2,1,0:T(8,128)(2,1)S(1)} %get-tuple-element.216), channel_id=1, source_target_pairs={{0,16},{16,32},{32,48},{48,64},{64,80},{80,96},{96,112},{112,128},... | collective-permute-start | bytes 589832 | tf_op jit(solution)/shard_map/while/body/eval_jaxpr/ppermute | solution.py:13
  108.7 7.3 %collective-permute-start = (bf16[24,32,128]{2,1,0:T(8,128)(2,1)S(1)}, bf16[24,32,128]{2,1,0:T(8,128)(2,1)S(1)}, u32[]{:S(2)}, u32[]{:S(2)}) collective-permute-start(bf16[24,32,128]{2,1,0:T(8,128)(2,1)S(1)} %get-tuple-element.216), channel_id=1, source_target_pairs={{0,16},{16,32},{32,48},{48,64},{64,80},{80,96},{96,112},{112,128},... | collective-permute-start | bytes 589832 | tf_op jit(solution)/shard_map/while/body/eval_jaxpr/ppermute | solution.py:13
  118.1 7.3 %collective-permute-start = (bf16[24,32,128]{2,1,0:T(8,128)(2,1)S(1)}, bf16[24,32,128]{2,1,0:T(8,128)(2,1)S(1)}, u32[]{:S(2)}, u32[]{:S(2)}) collective-permute-start(bf16[24,32,128]{2,1,0:T(8,128)(2,1)S(1)} %get-tuple-element.216), channel_id=1, source_target_pairs={{0,16},{16,32},{32,48},{48,64},{64,80},{80,96},{96,112},{112,128},... | collective-permute-start | bytes 589832 | tf_op jit(solution)/shard_map/while/body/eval_jaxpr/ppermute | solution.py:13
  127.4 7.4 %collective-permute-start = (bf16[24,32,128]{2,1,0:T(8,128)(2,1)S(1)}, bf16[24,32,128]{2,1,0:T(8,128)(2,1)S(1)}, u32[]{:S(2)}, u32[]{:S(2)}) collective-permute-start(bf16[24,32,128]{2,1,0:T(8,128)(2,1)S(1)} %get-tuple-element.216), channel_id=1, source_target_pairs={{0,16},{16,32},{32,48},{48,64},{64,80},{80,96},{96,112},{112,128},... | collective-permute-start | bytes 589832 | tf_op jit(solution)/shard_map/while/body/eval_jaxpr/ppermute | solution.py:13
  136.9 7.3 %collective-permute-start = (bf16[24,32,128]{2,1,0:T(8,128)(2,1)S(1)}, bf16[24,32,128]{2,1,0:T(8,128)(2,1)S(1)}, u32[]{:S(2)}, u32[]{:S(2)}) collective-permute-start(bf16[24,32,128]{2,1,0:T(8,128)(2,1)S(1)} %get-tuple-element.216), channel_id=1, source_target_pairs={{0,16},{16,32},{32,48},{48,64},{64,80},{80,96},{96,112},{112,128},... | collective-permute-start | bytes 589832 | tf_op jit(solution)/shard_map/while/body/eval_jaxpr/ppermute | solution.py:13
  146.3 7.2 %collective-permute-start = (bf16[24,32,128]{2,1,0:T(8,128)(2,1)S(1)}, bf16[24,32,128]{2,1,0:T(8,128)(2,1)S(1)}, u32[]{:S(2)}, u32[]{:S(2)}) collective-permute-start(bf16[24,32,128]{2,1,0:T(8,128)(2,1)S(1)} %get-tuple-element.216), channel_id=1, source_target_pairs={{0,16},{16,32},{32,48},{48,64},{64,80},{80,96},{96,112},{112,128},... | collective-permute-start | bytes 589832 | tf_op jit(solution)/shard_map/while/body/eval_jaxpr/ppermute | solution.py:13
  155.6 7.3 %collective-permute-start = (bf16[24,32,128]{2,1,0:T(8,128)(2,1)S(1)}, bf16[24,32,128]{2,1,0:T(8,128)(2,1)S(1)}, u32[]{:S(2)}, u32[]{:S(2)}) collective-permute-start(bf16[24,32,128]{2,1,0:T(8,128)(2,1)S(1)} %get-tuple-element.216), channel_id=1, source_target_pairs={{0,16},{16,32},{32,48},{48,64},{64,80},{80,96},{96,112},{112,128},... | collective-permute-start | bytes 589832 | tf_op jit(solution)/shard_map/while/body/eval_jaxpr/ppermute | solution.py:13
  164.9 7.3 %collective-permute-start = (bf16[24,32,128]{2,1,0:T(8,128)(2,1)S(1)}, bf16[24,32,128]{2,1,0:T(8,128)(2,1)S(1)}, u32[]{:S(2)}, u32[]{:S(2)}) collective-permute-start(bf16[24,32,128]{2,1,0:T(8,128)(2,1)S(1)} %get-tuple-element.216), channel_id=1, source_target_pairs={{0,16},{16,32},{32,48},{48,64},{64,80},{80,96},{96,112},{112,128},... | collective-permute-start | bytes 589832 | tf_op jit(solution)/shard_map/while/body/eval_jaxpr/ppermute | solution.py:13
  174.4 7.2 %collective-permute-start = (bf16[24,32,128]{2,1,0:T(8,128)(2,1)S(1)}, bf16[24,32,128]{2,1,0:T(8,128)(2,1)S(1)}, u32[]{:S(2)}, u32[]{:S(2)}) collective-permute-start(bf16[24,32,128]{2,1,0:T(8,128)(2,1)S(1)} %get-tuple-element.216), channel_id=1, source_target_pairs={{0,16},{16,32},{32,48},{48,64},{64,80},{80,96},{96,112},{112,128},... | collective-permute-start | bytes 589832 | tf_op jit(solution)/shard_map/while/body/eval_jaxpr/ppermute | solution.py:13
  183.7 7.3 %collective-permute-start = (bf16[24,32,128]{2,1,0:T(8,128)(2,1)S(1)}, bf16[24,32,128]{2,1,0:T(8,128)(2,1)S(1)}, u32[]{:S(2)}, u32[]{:S(2)}) collective-permute-start(bf16[24,32,128]{2,1,0:T(8,128)(2,1)S(1)} %get-tuple-element.216), channel_id=1, source_target_pairs={{0,16},{16,32},{32,48},{48,64},{64,80},{80,96},{96,112},{112,128},... | collective-permute-start | bytes 589832 | tf_op jit(solution)/shard_map/while/body/eval_jaxpr/ppermute | solution.py:13
  193.0 7.3 %collective-permute-start = (bf16[24,32,128]{2,1,0:T(8,128)(2,1)S(1)}, bf16[24,32,128]{2,1,0:T(8,128)(2,1)S(1)}, u32[]{:S(2)}, u32[]{:S(2)}) collective-permute-start(bf16[24,32,128]{2,1,0:T(8,128)(2,1)S(1)} %get-tuple-element.216), channel_id=1, source_target_pairs={{0,16},{16,32},{32,48},{48,64},{64,80},{80,96},{96,112},{112,128},... | collective-permute-start | bytes 589832 | tf_op jit(solution)/shard_map/while/body/eval_jaxpr/ppermute | solution.py:13
  202.3 7.3 %collective-permute-start = (bf16[24,32,128]{2,1,0:T(8,128)(2,1)S(1)}, bf16[24,32,128]{2,1,0:T(8,128)(2,1)S(1)}, u32[]{:S(2)}, u32[]{:S(2)}) collective-permute-start(bf16[24,32,128]{2,1,0:T(8,128)(2,1)S(1)} %get-tuple-element.216), channel_id=1, source_target_pairs={{0,16},{16,32},{32,48},{48,64},{64,80},{80,96},{96,112},{112,128},... | collective-permute-start | bytes 589832 | tf_op jit(solution)/shard_map/while/body/eval_jaxpr/ppermute | solution.py:13
  211.7 7.3 %collective-permute-start = (bf16[24,32,128]{2,1,0:T(8,128)(2,1)S(1)}, bf16[24,32,128]{2,1,0:T(8,128)(2,1)S(1)}, u32[]{:S(2)}, u32[]{:S(2)}) collective-permute-start(bf16[24,32,128]{2,1,0:T(8,128)(2,1)S(1)} %get-tuple-element.216), channel_id=1, source_target_pairs={{0,16},{16,32},{32,48},{48,64},{64,80},{80,96},{96,112},{112,128},... | collective-permute-start | bytes 589832 | tf_op jit(solution)/shard_map/while/body/eval_jaxpr/ppermute | solution.py:13
where the time goes:
time: 258 us; the launch traced here: 253 us
  waiting for transfers between devices  107 us (41%)
  other arithmetic  60 us (23%)
  local copies, waits for them, and re-layouts  56.5 us (22%)
  starting transfers between devices  20.7 us (8%)
  matrix products  8.19 us (3%)
    ppermute x15, waiting for transfers between devices, shifted(): return lax.ppermute(x, axis, [(i, (i + by) % peers) for i in range(peers)])  96.1 us
    transpose x1, other arithmetic, per_device(): filtered.transpose(1, 2, 0, 3).reshape(inputs * spectra_count, 2 * fine_len)  32.6 us
    dynamic_update_slice x16, other arithmetic, place(): lax.dynamic_update_slice_in_dim(totals, split_parts(products, inputs, spe...  18.4 us
    another operation x1, local copies, waits for them, and re-layouts, per_device(): return visibilities[None]  17.2 us
    transpose x1, local copies, waits for them, and re-layouts, per_device(): totals.transpose(1, 2, 3, 0, 4).reshape(RCAP, 2, inputs, stn_count * inputs)  15.1 us
    all_to_all x1, starting transfers between devices, per_device(): lax.all_to_all(outgoing, 'chan', split_axis=0, concat_axis=0, tiled=True)  11.8 us
    all_to_all x1, waiting for transfers between devices, per_device(): lax.all_to_all(outgoing, 'chan', split_axis=0, concat_axis=0, tiled=True)  11.1 us
    ppermute x15, starting transfers between devices, shifted(): return lax.ppermute(x, axis, [(i, (i + by) % peers) for i in range(peers)])  8.98 us
  transfers between devices with their start and end apart: 16, of which 16 were waited for; matrix products, arithmetic and copies ran while one was open for 0% of the time, Pallas kernels for 0%

commit v1 on v0

v1 whole, which is shorter than its diff:
```python
import functools
import math

import jax
import jax.numpy as jnp
from jax import lax
from jax.experimental import pallas as pl
from jax.experimental.pallas import tpu as pltpu
from jax.sharding import PartitionSpec as P

RCAP = 24
CAP = 2
FINE = 384
TAPS = 16
NSPEC = 32
KEEP = 8
NS = NSPEC + TAPS - 1
F32 = jnp.float32
BF16 = jnp.bfloat16
MESH = pl.DeviceIdType.MESH


def swap_halves(x):
    return pltpu.roll(x, 64, 1)


def trig_tables(chosen, branch):
    product = chosen * branch
    turns = jnp.floor((product + 0.5) * (1.0 / FINE))
    phase = product - turns * FINE
    quarter = jnp.floor((phase + (FINE // 8)) * (4.0 / FINE) + 1e-4)
    angle = (phase - quarter * (FINE // 4)) * (2.0 * math.pi / FINE)
    square = angle * angle
    sine = angle * (
        1.0
        + square
        * (-1.0 / 6 + square * (1.0 / 120 + square * (-1.0 / 5040 + square * (1.0 / 362880))))
    )
    cosine = 1.0 + square * (
        -0.5
        + square
        * (1.0 / 24 + square * (-1.0 / 720 + square * (1.0 / 40320 - square * (1.0 / 3628800))))
    )
    odd = (quarter == 1.0) | (quarter == 3.0)
    c = jnp.where(odd, sine, cosine)
    s = jnp.where(odd, cosine, sine)
    c = jnp.where((quarter == 1.0) | (quarter == 2.0), -c, c)
    s = jnp.where((quarter == 2.0) | (quarter == 3.0), -s, s)
    factor = 1.0 / math.sqrt(FINE)
    return ((c * factor).astype(BF16).astype(F32), (s * factor).astype(BF16).astype(F32))


CHUNKS = ((0, 12), (12, 24), (24, 36), (36, NS))


def channelise_kernel(
    survive_ref, owner_ref, taps_ref, volts_ref, out_ref, index_ref, buf, weights, partial, rows, sems
):
    band = lax.axis_index("chan")
    copies = []
    for n, (lo, hi) in enumerate(CHUNKS):
        copy = pltpu.make_async_copy(
            volts_ref.at[0, :, :, lo * FINE : hi * FINE],
            buf.at[:, :, lo * FINE : hi * FINE],
            sems.at[n],
        )
        copy.start()
        copies.append(copy)

    count = jnp.int32(0)
    for b in range(owner_ref.shape[0]):
        start = count
        for j in range(KEEP):
            hit = (owner_ref[b, j] == band).astype(jnp.int32)
            index_ref[jnp.minimum(count, RCAP)] = b * CAP + count - start
            count = count + hit
    index_ref[RCAP + 1] = count

    row = lax.broadcasted_iota(jnp.int32, (KEEP, FINE), 0)
    branch = lax.broadcasted_iota(jnp.int32, (KEEP, FINE), 1).astype(F32)
    chosen = jnp.zeros((KEEP, FINE), jnp.int32)
    for j in range(KEEP):
        chosen = jnp.where(row == j, survive_ref[band, j], chosen)
    cosine, sine = trig_tables(chosen.astype(F32), branch)
    both = jnp.concatenate([cosine, sine], 0)
    for p in range(TAPS):
        weights[p * 16 : (p + 1) * 16, :] = (both * taps_ref[p : p + 1, :]).astype(BF16)

    lane = lax.broadcasted_iota(jnp.int32, (KEEP, 128), 1)

    def finish(t):
        total = partial[t, 0:16, :]
        for p in range(1, TAPS):
            total = total + partial[t + p, p * 16 : (p + 1) * 16, :]
        swapped = swap_halves(total[8:16])
        rows[pl.ds(t, KEEP, stride=NSPEC), :] = total[0:8] + jnp.where(lane < 64, swapped, -swapped)

    done = 0
    for n, (lo, hi) in enumerate(CHUNKS):
        copies[n].wait()
        s = lo
        while s < hi:
            width = min(2, hi - s)
            block = jnp.concatenate(
                [
                    buf[:, :, (s + u) * FINE : (s + u + 1) * FINE].reshape(128, FINE)
                    for u in range(width)
                ],
                0,
            )
            product = lax.dot_general(
                weights[...], block, (((1,), (1,)), ((), ())), preferred_element_type=F32
            )
            for u in range(width):
                partial[s + u] = product[:, u * 128 : (u + 1) * 128]
            s += width
            while done + TAPS <= s and done < NSPEC:
                finish(done)
                done += 1

    out_ref[...] = jnp.zeros_like(out_ref)
    for j in range(KEEP):
        mine = owner_ref[band, j]
        rank = jnp.int32(0)
        for other in range(j):
            rank = rank + (owner_ref[band, other] == mine).astype(jnp.int32)
        out_ref[mine * CAP + rank] = rows[j * NSPEC : (j + 1) * NSPEC, :].astype(BF16)


def channelise(volts, taps, survive, owner):
    inputs = volts.shape[2]
    return pl.pallas_call(
        channelise_kernel,
        out_shape=(
            jax.ShapeDtypeStruct((owner.shape[0] * CAP, NSPEC, 2 * inputs), BF16),
            jax.ShapeDtypeStruct((RCAP + 8,), jnp.int32),
        ),
        in_specs=[
            pl.BlockSpec(memory_space=pltpu.SMEM),
            pl.BlockSpec(memory_space=pltpu.SMEM),
            pl.BlockSpec(memory_space=pltpu.VMEM),
            pl.BlockSpec(memory_space=pl.ANY),
        ],
        out_specs=(
            pl.BlockSpec(memory_space=pltpu.VMEM),
            pl.BlockSpec(memory_space=pltpu.SMEM),
        ),
        scratch_shapes=[
            pltpu.VMEM((2, inputs, NS * FINE), BF16),
            pltpu.VMEM((TAPS * 16, FINE), BF16),
            pltpu.VMEM((NS, TAPS * 16, 2 * inputs), F32),
            pltpu.VMEM((KEEP * NSPEC, 2 * inputs), F32),
            pltpu.SemaphoreType.DMA((len(CHUNKS),)),
        ],
        compiler_params=pltpu.CompilerParams(vmem_limit_bytes=58 << 20),
        name="channelise",
    )(survive, owner, taps, volts)


KCH = 4
PER = RCAP // KCH
OWN, Y0, R0, L0, R1, L1, F0, F1 = range(8)


def exchange_kernel(
    index_ref, out_ref, gathered, arrived, send1, recv1, send2, recv2, sib_send, sib_recv
):
    stn = lax.axis_index("stn")
    chan = lax.axis_index("chan")
    nchan = lax.axis_size("chan")
    x, y, core = stn // 4, (stn // 2) % 2, stn % 2

    def name(dx, dy, dcore=0):
        return ((x + dx) % 4) * 4 + ((y + dy) % 2) * 2 + (core + dcore) % 2

    places = {
        OWN: (0, 0), Y0: (0, 1), R0: (1, 0), L0: (3, 0), R1: (1, 1), L1: (3, 1), F0: (2, 0), F1: (2, 1)
    }
    right, left, across, sibling = name(1, 0), name(3, 0), name(0, 1), name(0, 0, 1)

    barrier = pltpu.get_barrier_semaphore()
    for other in (right, left, across, sibling):
        pl.semaphore_signal(
            barrier, inc=1, device_id={"stn": other, "chan": chan}, device_id_type=MESH
        )
    for step in range(1, nchan):
        pl.semaphore_signal(
            barrier,
            inc=1,
            device_id={"stn": stn, "chan": (chan + step) % nchan},
            device_id_type=MESH,
        )
    pl.semaphore_wait(barrier, 4 + nchan - 1)

    def turn(step):
        to = (chan + step) % nchan
        return pltpu.make_async_remote_copy(
            src_ref=out_ref.at[pl.ds(to * CAP, CAP)],
            dst_ref=arrived.at[pl.ds(chan * CAP, CAP)],
            send_sem=send1.at[step],
            recv_sem=recv1.at[step],
            device_id={"stn": stn, "chan": to},
            device_id_type=MESH,
        )

    order = [s for d in range(nchan // 2, 0, -1) for s in sorted({d, nchan - d})]
    turns = {s: turn(s) for s in order}
    for s in order:
        turns[s].start()
    arrived[pl.ds(chan * CAP, CAP)] = out_ref[pl.ds(chan * CAP, CAP)]
    for s in order:
        turns[s].wait_recv()

    count = index_ref[RCAP + 1]
    for r in range(RCAP):
        block = arrived[index_ref[r] % (nchan * CAP)]
        gathered[stn, r] = jnp.where(r < count, block, jnp.zeros_like(block))

    sends = []

    def part(block, k):
        dx, dy = places[block]
        return gathered.at[name(dx, dy), pl.ds(k * PER, PER)]

    def push(block, k, to, slot):
        copy = pltpu.make_async_remote_copy(
            src_ref=part(block, k),
            dst_ref=part(block, k),
            send_sem=send2.at[slot, k],
            recv_sem=recv2.at[slot, k],
            device_id={"stn": to, "chan": chan},
            device_id_type=MESH,
        )
        copy.start()
        sends.append(copy)

    def share(block, k):
        copy = pltpu.make_async_remote_copy(
            src_ref=part(block, k),
            dst_ref=part(block, k),
            send_sem=sib_send.at[block, k],
            recv_sem=sib_recv.at[block, k],
            device_id={"stn": sibling, "chan": chan},
            device_id_type=MESH,
        )
        copy.start()
        sends.append(copy)

    def arrive(block, k):
        pltpu.make_async_remote_copy(
            src_ref=part(block, k),
            dst_ref=part(block, k),
            send_sem=send2.at[block, k],
            recv_sem=recv2.at[block, k],
            device_id={"stn": right, "chan": chan},
            device_id_type=MESH,
        ).wait_recv()

    for k in range(KCH):
        push(OWN, k, across, Y0)
        push(OWN, k, right, L0)
        push(OWN, k, left, R0)
        share(OWN, k)
    for k in range(KCH):
        arrive(Y0, k)
        push(Y0, k, right, L1)
        push(Y0, k, left, R1)
        share(Y0, k)
        arrive(R0, k)
        if k < KCH // 2:
            push(R0, k, left, F0)
        share(R0, k)
        arrive(L0, k)
        if k >= KCH // 2:
            push(L0, k, right, F0)
        share(L0, k)
    for k in (v for pair in zip(range(KCH // 2), range(KCH // 2, KCH)) for v in pair):
        arrive(F0, k)
        push(F0, k, across, F1)
        share(F0, k)
    for k in range(KCH):
        arrive(R1, k)
        share(R1, k)
        arrive(L1, k)
        share(L1, k)
    for k in range(KCH):
        arrive(F1, k)
        share(F1, k)
    for block in range(8):
        dx, dy = places[block]
        for k in range(KCH):
            ref = gathered.at[name(dx, dy, 1), pl.ds(k * PER, PER)]
            pltpu.make_async_remote_copy(
                src_ref=ref,
                dst_ref=ref,
                send_sem=sib_send.at[block, k],
                recv_sem=sib_recv.at[block, k],
                device_id={"stn": sibling, "chan": chan},
                device_id_type=MESH,
            ).wait_recv()
    for s in order:
        turns[s].wait_send()
    for copy in sends:
        copy.wait_send()


def exchange(index, outgoing, stn_count):
    slots, spectra, lanes = outgoing.shape
    return pl.pallas_call(
        exchange_kernel,
        out_shape=jax.ShapeDtypeStruct((stn_count, RCAP, spectra, lanes), BF16),
        in_specs=[
            pl.BlockSpec(memory_space=pltpu.SMEM),
            pl.BlockSpec(memory_space=pltpu.VMEM),
        ],
        out_specs=pl.BlockSpec(memory_space=pltpu.VMEM),
        scratch_shapes=[
            pltpu.VMEM((slots, spectra, lanes), BF16),
            pltpu.SemaphoreType.DMA((slots // CAP,)),
            pltpu.SemaphoreType.DMA((slots // CAP,)),
            pltpu.SemaphoreType.DMA((8, KCH)),
            pltpu.SemaphoreType.DMA((8, KCH)),
            pltpu.SemaphoreType.DMA((8, KCH)),
            pltpu.SemaphoreType.DMA((8, KCH)),
        ],
        compiler_params=pltpu.CompilerParams(
            collective_id=0, has_side_effects=True, vmem_limit_bytes=16 << 20
        ),
        name="exchange",
    )(index, outgoing)


SLOTS_STEP = 2


def correlate_kernel(stn_count, spectra_count, gathered, out_ref):
    stn = lax.axis_index("stn")
    step = pl.program_id(0)
    lane = lax.broadcasted_iota(jnp.int32, (spectra_count, 128), 1)
    low = lane < 64
    for u in range(SLOTS_STEP):
        slot = step * SLOTS_STEP + u
        own = gathered[stn, slot].astype(F32) * (1.0 / spectra_count)
        turned = swap_halves(own)
        turned = jnp.where(low, turned, -turned)
        left = jnp.concatenate([own, turned], 0).astype(BF16)
        for n in range(0, stn_count, 2):
            first = gathered[n, slot].astype(F32)
            second = gathered[n + 1, slot].astype(F32)
            real = jnp.where(low, first, swap_halves(second))
            imag = jnp.where(low, swap_halves(first), second)
            block = jnp.concatenate([real, imag], 0).astype(BF16)
            product = lax.dot_general(
                left, block, (((0,), (0,)), ((), ())), preferred_element_type=F32
            )
            out_ref[0, u, :, :, n * 64 : (n + 2) * 64] = product.astype(BF16).reshape(2, 64, 128)


def correlate(gathered):
    stn_count, slots, spectra, lanes = gathered.shape
    inputs = lanes // 2
    return pl.pallas_call(
        functools.partial(correlate_kernel, stn_count, spectra),
        grid=(slots // SLOTS_STEP,),
        out_shape=jax.ShapeDtypeStruct((1, slots, 2, inputs, stn_count * inputs), BF16),
        in_specs=[pl.BlockSpec(memory_space=pltpu.VMEM)],
        out_specs=pl.BlockSpec(
            (1, SLOTS_STEP, 2, inputs, stn_count * inputs), lambda i: (0, i, 0, 0, 0)
        ),
        compiler_params=pltpu.CompilerParams(vmem_limit_bytes=16 << 20),
        name="correlate",
    )(gathered)


def per_device(volts, taps, survive, owner):
    outgoing, index = channelise(volts, taps, survive, owner)
    gathered = exchange(index, outgoing, lax.axis_size("stn"))
    return correlate(gathered)


def solution(mesh):
    return jax.shard_map(
        per_device,
        mesh=mesh,
        in_specs=(P("chan", None, "stn", None), P(), P(), P()),
        out_specs=P("chan", None, None, "stn", None),
        check_vma=False,
    )
```

time: 258 us -> 56.3 us (0.22); the launches traced: 253 us -> 56 us
  waiting for transfers between devices: 107 us -> 0 us
  other arithmetic: 60 us -> 0 us
  local copies, waits for them, and re-layouts: 56.5 us -> 4.25 us
  Pallas kernels: 0 us -> 51.8 us
  starting transfers between devices: 20.7 us -> 0 us
  matrix products: 8.19 us -> 0 us
    ppermute x15 -> x0, waiting for transfers between devices: 96.1 us -> none  [shifted(): return lax.ppermute(x, axis, [(i, (i + by) % peers) for i in range(peers)])]
    pallas_call x0 -> x3, Pallas kernels: none -> 51.8 us  [the longest x1 38.5 us: exchange(): pl.pallas_call(exchange_kernel, out_shape=jax.ShapeDtypeStruct((stn_count...]
    transpose x1 -> x0, other arithmetic: 32.6 us -> none  [per_device(): filtered.transpose(1, 2, 0, 3).reshape(inputs * spectra_count, 2 * fine_len)]
    another operation x2 -> x0, local copies, waits for them, and re-layouts: 25 us -> none  [the longest x1 17.2 us: per_device(): return visibilities[None]]
    transpose x3 -> x0, local copies, waits for them, and re-layouts: 18.5 us -> none  [the longest x1 15.1 us: per_device(): totals.transpose(1, 2, 3, 0, 4).reshape(RCAP, 2, inputs, stn_count * inputs)]
    dynamic_update_slice x16 -> x0, other arithmetic: 18.4 us -> none  [place(): lax.dynamic_update_slice_in_dim(totals, split_parts(products, inputs, spe...]
    all_to_all x1 -> x0, starting transfers between devices: 11.8 us -> none  [per_device(): lax.all_to_all(outgoing, 'chan', split_axis=0, concat_axis=0, tiled=True)]
    all_to_all x1 -> x0, waiting for transfers between devices: 11.1 us -> none  [per_device(): lax.all_to_all(outgoing, 'chan', split_axis=0, concat_axis=0, tiled=True)]
  transfers between devices with their start and end apart: 16 -> 0, of which waited for: 16 -> 0; matrix products, arithmetic and copies ran while one was open for 0% -> 0% of each run, Pallas kernels for 0% -> 0%
where the time goes in v1:
time: 56.3 us; the launch traced here: 56 us
  Pallas kernels  51.8 us (92%)
  local copies, waits for them, and re-layouts  4.25 us (8%)
    pallas_call x1, Pallas kernels, exchange(): pl.pallas_call(exchange_kernel, out_shape=jax.ShapeDtypeStruct((stn_count...  38.5 us
    pallas_call x1, Pallas kernels, correlate(): pl.pallas_call(functools.partial(correlate_kernel, stn_count, spectra), g...  7.67 us
    pallas_call x1, Pallas kernels, channelise(): pl.pallas_call(channelise_kernel, out_shape=(jax.ShapeDtypeStruct((owner....  5.59 us
    unnamed x6, local copies, waits for them, and re-layouts  4.25 us

profile of v1, /device:TPU:1, one launch (start us, length us, event | category | flops | bytes accessed | tf_op | source)
XLA Modules:
  0.0 56.0 jit_solution(13360547840472530146)
XLA Ops:
  0.0 1.4 %copy.5.survive_ref = s32[16,8]{1,0:T(8,128)} copy(s32[16,8]{0,1:T(8,128)} %param.6) | data formatting | bytes 1024 | tf_op args[2]
  1.4 1.3 %copy.6.owner_ref = s32[16,8]{1,0:T(8,128)} copy(s32[16,8]{0,1:T(8,128)} %param.7) | data formatting | bytes 1024 | tf_op args[3]
  2.7 5.6 %channelise.1 = (bf16[32,32,128]{2,1,0:T(8,128)(2,1)}, s32[32]{0:T(128)}) custom-call(s32[16,8]{1,0:T(8,128)} %copy.5.survive_ref, s32[16,8]{1,0:T(8,128)} %copy.6.owner_ref, f32[16,384]{1,0:T(8,128)} %taps_ref.1, bf16[1,2,64,18048]{3,2,1,0:T(8,128)(2,1)} %volts_ref.1), custom_call_target="tpu_custom_call" | custom-call | tf_op jit(solution)/shard_map/channelise/pallas_call | solution.py:132
  8.3 0.0 copy-start
  8.3 0.9 %copy-done = bf16[32,32,128]{2,1,0:T(8,128)(2,1)S(1)} copy-done((bf16[32,32,128]{2,1,0:T(8,128)(2,1)S(1)}, bf16[32,32,128]{2,1,0:T(8,128)(2,1)}, u32[]{:S(2)}) %copy-start) | copy-done | bytes 262168
  9.3 0.0 copy-start.1
  9.3 0.6 %copy-done.1 = s32[32]{0:T(128)S(1)} copy-done((s32[32]{0:T(128)S(1)}, s32[32]{0:T(128)}, u32[]{:S(2)}) %copy-start.1) | copy-done | bytes 152
  9.9 38.5 %exchange.1.gathered = bf16[16,24,32,128]{3,2,1,0:T(8,128)(2,1)S(1)} custom-call(s32[32]{0:T(128)S(1)} %copy-done.1, bf16[32,32,128]{2,1,0:T(8,128)(2,1)S(1)} %copy-done), custom_call_target="tpu_custom_call" | custom-call | tf_op jit(solution)/shard_map/exchange/pallas_call | solution.py:309
  48.4 7.7 %correlate.1 = bf16[1,24,2,64,1024]{4,3,2,1,0:T(8,128)(2,1)} custom-call(bf16[16,24,32,128]{3,2,1,0:T(8,128)(2,1)S(1)} %exchange.1.gathered), custom_call_target="tpu_custom_call" | custom-call | tf_op jit(solution)/shard_map/correlate/pallas_call | solution.py:362
Async XLA Ops:
  8.3 1.0 %copy-start = (bf16[32,32,128]{2,1,0:T(8,128)(2,1)S(1)}, bf16[32,32,128]{2,1,0:T(8,128)(2,1)}, u32[]{:S(2)}) copy-start(bf16[32,32,128]{2,1,0:T(8,128)(2,1)} %get-tuple-element.8.out_ref) | copy-start | bytes 786436
  9.3 0.6 %copy-start.1 = (s32[32]{0:T(128)S(1)}, s32[32]{0:T(128)}, u32[]{:S(2)}) copy-start(s32[32]{0:T(128)} %get-tuple-element.7.index_ref) | copy-start | bytes 388

commit v2 on v1

v2 whole, which is shorter than its diff:
```python
import functools
import math

import jax
import jax.numpy as jnp
from jax import lax
from jax.experimental import pallas as pl
from jax.experimental.pallas import tpu as pltpu
from jax.sharding import PartitionSpec as P

RCAP = 24
CAP = 2
FINE = 384
TAPS = 16
NSPEC = 32
KEEP = 8
NS = NSPEC + TAPS - 1
F32 = jnp.float32
BF16 = jnp.bfloat16
MESH = pl.DeviceIdType.MESH


def swap_halves(x):
    return pltpu.roll(x, 64, 1)


def trig_tables(chosen, branch):
    product = chosen * branch
    turns = jnp.floor((product + 0.5) * (1.0 / FINE))
    phase = product - turns * FINE
    quarter = jnp.floor((phase + (FINE // 8)) * (4.0 / FINE) + 1e-4)
    angle = (phase - quarter * (FINE // 4)) * (2.0 * math.pi / FINE)
    square = angle * angle
    sine = angle * (
        1.0
        + square
        * (-1.0 / 6 + square * (1.0 / 120 + square * (-1.0 / 5040 + square * (1.0 / 362880))))
    )
    cosine = 1.0 + square * (
        -0.5
        + square
        * (1.0 / 24 + square * (-1.0 / 720 + square * (1.0 / 40320 - square * (1.0 / 3628800))))
    )
    odd = (quarter == 1.0) | (quarter == 3.0)
    c = jnp.where(odd, sine, cosine)
    s = jnp.where(odd, cosine, sine)
    c = jnp.where((quarter == 1.0) | (quarter == 2.0), -c, c)
    s = jnp.where((quarter == 2.0) | (quarter == 3.0), -s, s)
    factor = 1.0 / math.sqrt(FINE)
    return ((c * factor).astype(BF16).astype(F32), (s * factor).astype(BF16).astype(F32))


STEP = 4
STEPS = (NS + STEP) // STEP
HALVES = 2
HALF = NSPEC // HALVES
KS = 2
PER = RCAP // KS
KCH = HALVES * KS
OWN, Y0, R0, L0, R1, L1, F0, F1 = range(8)
PLACES = {
    OWN: (0, 0), Y0: (0, 1), R0: (1, 0), L0: (3, 0), R1: (1, 1), L1: (3, 1), F0: (2, 0), F1: (2, 1)
}


def front_kernel(
    survive_ref, owner_ref, taps_ref, volts_ref, gathered,
    buf, weights, partial, rows, channels, outbox, arrived0, arrived1, pick, source,
    load_sem, send1, recv1, send2, recv2, sib_send, sib_recv,
):
    arrived = (arrived0, arrived1)
    stn = lax.axis_index("stn")
    chan = lax.axis_index("chan")
    nchan = lax.axis_size("chan")
    x, y, core = stn // 4, (stn // 2) % 2, stn % 2

    def name(dx, dy, dcore=0):
        return ((x + dx) % 4) * 4 + ((y + dy) % 2) * 2 + (core + dcore) % 2

    right, left, across, sibling = name(1, 0), name(3, 0), name(0, 1), name(0, 0, 1)

    def load(n, width=STEP):
        lanes = pl.ds(pl.multiple_of(n * (STEP * FINE), 128), width * FINE)
        return pltpu.make_async_copy(
            volts_ref.at[0, :, :, lanes], buf.at[:, :, lanes], load_sem.at[n]
        )

    last = NS - (STEPS - 1) * STEP

    @pl.loop(0, STEPS - 1)
    def _(n):
        load(n).start()

    load(STEPS - 1, last).start()

    barrier = pltpu.get_barrier_semaphore()
    for other in (right, left, across, sibling):
        pl.semaphore_signal(
            barrier, inc=1, device_id={"stn": other, "chan": chan}, device_id_type=MESH
        )

    @pl.loop(1, nchan)
    def _(step):
        pl.semaphore_signal(
            barrier,
            inc=1,
            device_id={"stn": stn, "chan": (chan + step) % nchan},
            device_id_type=MESH,
        )

    row = lax.broadcasted_iota(jnp.int32, (KEEP, FINE), 0)
    branch = lax.broadcasted_iota(jnp.int32, (KEEP, FINE), 1).astype(F32)
    chosen = jnp.zeros((KEEP, FINE), jnp.int32)
    for j in range(KEEP):
        chosen = jnp.where(row == j, survive_ref[j, chan], chosen)
    cosine, sine = trig_tables(chosen.astype(F32), branch)
    both = jnp.concatenate([cosine, sine], 0)
    for p in range(TAPS):
        weights[p * 16 : (p + 1) * 16, :] = (both * taps_ref[p : p + 1, :]).astype(BF16)

    targets = []
    owners = [owner_ref[j, chan] for j in range(KEEP)]
    for j in range(KEEP):
        rank = jnp.int32(0)
        for other in range(j):
            rank = rank + (owners[other] == owners[j]).astype(jnp.int32)
        targets.append(owners[j] * CAP + rank)

    @pl.loop(0, nchan * CAP)
    def _(slot):
        found = jnp.int32(0)
        for j in range(1, KEEP):
            found = jnp.where(targets[j] == slot, j, found)
        pick[slot] = found

    def transform(n):
        at = n * (STEP * FINE)
        for pair in range(STEP // 2):
            block = jnp.concatenate(
                [
                    buf[:, :, pl.ds(pl.multiple_of(at + (pair * 2 + u) * FINE, 128), FINE)].reshape(
                        128, FINE
                    )
                    for u in range(2)
                ],
                0,
            )
            product = lax.dot_general(
                weights[...], block, (((1,), (1,)), ((), ())), preferred_element_type=F32
            )
            for u in range(2):
                partial[n * STEP + pair * 2 + u] = product[:, u * 128 : (u + 1) * 128]

    lane = lax.broadcasted_iota(jnp.int32, (KEEP, 128), 1)

    def turn(half, step):
        to = (chan + step) % nchan
        return pltpu.make_async_remote_copy(
            src_ref=outbox.at[half, pl.ds(to * CAP, CAP)],
            dst_ref=arrived[half].at[pl.ds(chan * CAP, CAP)],
            send_sem=send1.at[half, step],
            recv_sem=recv1.at[half, step],
            device_id={"stn": stn, "chan": to},
            device_id_type=MESH,
        )

    done = 0
    for half in range(HALVES):
        upto = ((half + 1) * HALF + TAPS - 1 + STEP - 1) // STEP

        @pl.loop(done, upto)
        def _(n):
            @pl.when(n < STEPS - 1)
            def _():
                load(n).wait()

            @pl.when(n == STEPS - 1)
            def _():
                load(STEPS - 1, last).wait()

            transform(n)

        done = upto

        @pl.loop(0, HALF)
        def _(t):
            at = half * HALF + t
            total = partial[at, 0:16, :]
            for p in range(1, TAPS):
                total = total + partial[at + p, p * 16 : (p + 1) * 16, :]
            swapped = swap_halves(total[8:16])
            rows[pl.ds(t, KEEP, stride=HALF), :] = total[0:8] + jnp.where(
                lane < 64, swapped, -swapped
            )

        for j in range(KEEP):
            channels[j] = rows[j * HALF : (j + 1) * HALF, :].astype(BF16)

        @pl.loop(0, nchan * CAP)
        def _(slot):
            outbox[half, slot] = channels[pick[slot]]

        if half == 0:
            pl.semaphore_wait(barrier, 4 + nchan - 1)

        @pl.loop(0, nchan - 1)
        def _(i):
            turn(half, nchan // 2 + ((i + 1) // 2) * (2 * (i % 2) - 1)).start()

        arrived[half][pl.ds(chan * CAP, CAP)] = outbox[half, pl.ds(chan * CAP, CAP)]

    counts = []
    count = jnp.int32(0)
    for b in range(nchan):
        for j in range(KEEP):
            count = count + (owner_ref[j, b] == chan).astype(jnp.int32)
        counts.append(count)

    @pl.loop(0, RCAP)
    def _(r):
        skip = jnp.int32(0)
        for b in range(nchan):
            skip = jnp.where(counts[b] <= r, (b + 1) * CAP - counts[b], skip)
        source[r] = jnp.minimum(r + skip, nchan * CAP - 1)

    sends = []

    def part(block, k):
        dx, dy = PLACES[block]
        return gathered.at[k // KS, name(dx, dy), pl.ds((k % KS) * PER, PER)]

    def whole(block, half, dcore=0):
        dx, dy = PLACES[block]
        return gathered.at[half, name(dx, dy, dcore)]

    def push(block, k, to, slot):
        copy = pltpu.make_async_remote_copy(
            src_ref=part(block, k),
            dst_ref=part(block, k),
            send_sem=send2.at[slot, k],
            recv_sem=recv2.at[slot, k],
            device_id={"stn": to, "chan": chan},
            device_id_type=MESH,
        )
        copy.start()
        sends.append(copy)

    def share(block, k):
        if k % KS < KS - 1:
            return
        copy = pltpu.make_async_remote_copy(
            src_ref=whole(block, k // KS),
            dst_ref=whole(block, k // KS),
            send_sem=sib_send.at[block, k // KS],
            recv_sem=sib_recv.at[block, k // KS],
            device_id={"stn": sibling, "chan": chan},
            device_id_type=MESH,
        )
        copy.start()
        sends.append(copy)

    def arrive(block, k):
        pltpu.make_async_remote_copy(
            src_ref=part(block, k),
            dst_ref=part(block, k),
            send_sem=send2.at[block, k],
            recv_sem=recv2.at[block, k],
            device_id={"stn": right, "chan": chan},
            device_id_type=MESH,
        ).wait_recv()

    for half in range(HALVES):

        @pl.loop(1, nchan)
        def _(step):
            turn(half, step).wait_recv()

        @pl.loop(0, RCAP)
        def _(r):
            block = arrived[half][source[r]]
            gathered[half, stn, r] = jnp.where(r < count, block, jnp.zeros_like(block))

        for k in range(half * KS, (half + 1) * KS):
            push(OWN, k, right, L0)
            push(OWN, k, left, R0)
            push(OWN, k, across, Y0)
            share(OWN, k)

    def far(k):
        arrive(F0, k)
        push(F0, k, across, F1)
        share(F0, k)

    for k in range(KCH):
        arrive(R0, k)
        if k % 2 == 0:
            push(R0, k, left, F0)
        arrive(L0, k)
        if k % 2 == 1:
            push(L0, k, right, F0)
        arrive(Y0, k)
        push(Y0, k, right, L1)
        push(Y0, k, left, R1)
        for block in (R0, L0, Y0):
            share(block, k)
        if k >= 2:
            far(k - 2)
    for k in range(KCH - 2, KCH):
        far(k)
    for k in range(KCH):
        arrive(R1, k)
        share(R1, k)
        arrive(L1, k)
        share(L1, k)
    for k in range(KCH):
        arrive(F1, k)
        share(F1, k)
    for block in range(8):
        for half in range(HALVES):
            pltpu.make_async_remote_copy(
                src_ref=whole(block, half, 1),
                dst_ref=whole(block, half, 1),
                send_sem=sib_send.at[block, half],
                recv_sem=sib_recv.at[block, half],
                device_id={"stn": sibling, "chan": chan},
                device_id_type=MESH,
            ).wait_recv()
    for half in range(HALVES):

        @pl.loop(1, nchan)
        def _(step):
            turn(half, step).wait_send()

    for copy in sends:
        copy.wait_send()


def front(volts, taps, survive, owner, stn_count):
    inputs = volts.shape[2]
    lanes = 2 * inputs
    nchan = owner.shape[1]
    dma = pltpu.SemaphoreType.DMA
    return pl.pallas_call(
        front_kernel,
        out_shape=jax.ShapeDtypeStruct((HALVES, stn_count, RCAP, HALF, lanes), BF16),
        in_specs=[
            pl.BlockSpec(memory_space=pltpu.SMEM),
            pl.BlockSpec(memory_space=pltpu.SMEM),
            pl.BlockSpec(memory_space=pltpu.VMEM),
            pl.BlockSpec(memory_space=pltpu.HBM),
        ],
        out_specs=pl.BlockSpec(memory_space=pltpu.VMEM),
        scratch_shapes=[
            pltpu.VMEM((2, inputs, STEPS * STEP * FINE), BF16),
            pltpu.VMEM((TAPS * 16, FINE), BF16),
            pltpu.VMEM((STEPS * STEP, TAPS * 16, lanes), F32),
            pltpu.VMEM((KEEP * HALF, lanes), F32),
            pltpu.VMEM((KEEP, HALF, lanes), BF16),
            pltpu.VMEM((HALVES, nchan * CAP, HALF, lanes), BF16),
            pltpu.VMEM((nchan * CAP, HALF, lanes), BF16),
            pltpu.VMEM((nchan * CAP, HALF, lanes), BF16),
            pltpu.SMEM((nchan * CAP,), jnp.int32),
            pltpu.SMEM((RCAP,), jnp.int32),
            dma((STEPS,)),
            dma((HALVES, nchan)),
            dma((HALVES, nchan)),
            dma((8, KCH)),
            dma((8, KCH)),
            dma((8, HALVES)),
            dma((8, HALVES)),
        ],
        compiler_params=pltpu.CompilerParams(
            collective_id=0, has_side_effects=True, vmem_limit_bytes=48 << 20
        ),
        name="front",
    )(survive, owner, taps, volts)


def correlate_kernel(stn_count, gathered, out_ref, built, sems):
    stn = lax.axis_index("stn")
    low = lax.broadcasted_iota(jnp.int32, (NSPEC, 128), 1) < 64

    def series(n, slot):
        return jnp.concatenate([gathered[h, n, slot] for h in range(HALVES)], 0).astype(F32)

    def store(slot):
        return pltpu.make_async_copy(built.at[slot], out_ref.at[0, slot], sems.at[slot])

    @pl.loop(0, RCAP)
    def _(slot):
        own = series(stn, slot) * (1.0 / NSPEC)
        turned = swap_halves(own)
        turned = jnp.where(low, turned, -turned)
        left = jnp.concatenate([own, turned], 0).astype(BF16)
        for n in range(0, stn_count, 4):
            columns = []
            for m in range(n, n + 4, 2):
                first, second = series(m, slot), series(m + 1, slot)
                real = jnp.where(low, first, swap_halves(second))
                imag = jnp.where(low, swap_halves(first), second)
                columns.append(jnp.concatenate([real, imag], 0).astype(BF16))
            product = lax.dot_general(
                left,
                jnp.concatenate(columns, 1),
                (((0,), (0,)), ((), ())),
                preferred_element_type=F32,
            )
            built[slot, :, :, n * 64 : (n + 4) * 64] = product.astype(BF16).reshape(2, 64, 256)
        store(slot).start()

    @pl.loop(0, RCAP)
    def _(slot):
        store(slot).wait()


def correlate(gathered):
    stn_count, lanes = gathered.shape[1], gathered.shape[4]
    inputs = lanes // 2
    return pl.pallas_call(
        functools.partial(correlate_kernel, stn_count),
        out_shape=jax.ShapeDtypeStruct((1, RCAP, 2, inputs, stn_count * inputs), BF16),
        in_specs=[pl.BlockSpec(memory_space=pltpu.VMEM)],
        out_specs=pl.BlockSpec(memory_space=pltpu.HBM),
        scratch_shapes=[
            pltpu.VMEM((RCAP, 2, inputs, stn_count * inputs), BF16),
            pltpu.SemaphoreType.DMA((RCAP,)),
        ],
        compiler_params=pltpu.CompilerParams(vmem_limit_bytes=16 << 20),
        name="correlate",
    )(gathered)


def per_device(volts, taps, survive, owner):
    gathered = front(volts, taps, survive.T, owner.T, lax.axis_size("stn"))
    return correlate(gathered)


def solution(mesh):
    return jax.shard_map(
        per_device,
        mesh=mesh,
        in_specs=(P("chan", None, "stn", None), P(), P(), P()),
        out_specs=P("chan", None, None, "stn", None),
        check_vma=False,
    )
```

time: 56.3 us -> 50.1 us (0.89)
  Pallas kernels: 51.8 us -> 47.8 us
  local copies, waits for them, and re-layouts: 4.25 us -> 2.11 us
    pallas_call x3 -> x2, Pallas kernels: 51.8 us -> 47.8 us  [the longest x1 38.9 us: front(): pl.pallas_call(front_kernel, out_shape=jax.ShapeDtypeStruct((HALVES, stn_...]
    unnamed x6, local copies, waits for them, and re-layouts: 4.25 us -> 2.11 us
where the time goes in v2:
time: 50.1 us; the launch traced here: 49.9 us
  Pallas kernels  47.8 us (95%)
  local copies, waits for them, and re-layouts  2.11 us (4%)
    pallas_call x1, Pallas kernels, front(): pl.pallas_call(front_kernel, out_shape=jax.ShapeDtypeStruct((HALVES, stn_...  38.9 us
    pallas_call x1, Pallas kernels, correlate(): pl.pallas_call(functools.partial(correlate_kernel, stn_count), out_shape=...  8.88 us
    unnamed x6, local copies, waits for them, and re-layouts  2.11 us

profile of v2, /device:TPU:1, one launch (start us, length us, event | category | flops | bytes accessed | tf_op | source)
XLA Modules:
  0.0 49.9 jit_solution(8359931237686304802)
XLA Ops:
  0.0 0.0 copy-start
  0.0 0.7 %copy-done = f32[16,384]{1,0:T(8,128)S(1)} copy-done((f32[16,384]{1,0:T(8,128)S(1)}, f32[16,384]{1,0:T(8,128)}, u32[]{:S(2)}) %copy-start) | copy-done | bytes 24600
  0.7 0.0 copy-start.1
  0.7 0.7 %copy-done.1 = s32[16,8]{0,1:T(8,128)S(1)} copy-done((s32[16,8]{0,1:T(8,128)S(1)}, s32[16,8]{0,1:T(8,128)}, u32[]{:S(2)}) %copy-start.1) | copy-done | bytes 536
  1.4 0.0 copy-start.2
  1.4 0.7 %copy-done.2 = s32[16,8]{0,1:T(8,128)S(1)} copy-done((s32[16,8]{0,1:T(8,128)S(1)}, s32[16,8]{0,1:T(8,128)}, u32[]{:S(2)}) %copy-start.2) | copy-done | bytes 536
  2.1 38.9 %front.1.gathered = bf16[2,16,24,16,128]{4,3,2,1,0:T(8,128)(2,1)S(1)} custom-call(s32[8,16]{1,0:T(8,128)S(1)} %bitcast.2, s32[8,16]{1,0:T(8,128)S(1)} %bitcast.3, f32[16,384]{1,0:T(8,128)S(1)} %copy-done, bf16[1,2,64,18048]{3,2,1,0:T(8,128)(2,1)} %volts_ref.1), custom_call_target="tpu_custom_call" | custom-call | tf_op jit(solution)/shard_map/front/pallas_call | solution.py:343
  41.0 8.9 %correlate.1 = bf16[1,24,2,64,1024]{4,3,2,1,0:T(8,128)(2,1)} custom-call(bf16[2,16,24,16,128]{4,3,2,1,0:T(8,128)(2,1)S(1)} %front.1.gathered), custom_call_target="tpu_custom_call" | custom-call | tf_op jit(solution)/shard_map/correlate/pallas_call | solution.py:419
Async XLA Ops:
  0.0 0.7 %copy-start = (f32[16,384]{1,0:T(8,128)S(1)}, f32[16,384]{1,0:T(8,128)}, u32[]{:S(2)}) copy-start(f32[16,384]{1,0:T(8,128)} %taps_ref.1) | copy-start | bytes 73732
  0.7 0.7 %copy-start.1 = (s32[16,8]{0,1:T(8,128)S(1)}, s32[16,8]{0,1:T(8,128)}, u32[]{:S(2)}) copy-start(s32[16,8]{0,1:T(8,128)} %param.6) | copy-start | bytes 1540
  1.4 0.7 %copy-start.2 = (s32[16,8]{0,1:T(8,128)S(1)}, s32[16,8]{0,1:T(8,128)}, u32[]{:S(2)}) copy-start(s32[16,8]{0,1:T(8,128)} %param.7) | copy-start | bytes 1540

commit v3 on v2

--- a/solution.py
+++ b/solution.py
@@ -50,8 +50,8 @@
     return ((c * factor).astype(BF16).astype(F32), (s * factor).astype(BF16).astype(F32))
 
 
-STEP = 4
-STEPS = (NS + STEP) // STEP
+CHUNKS = ((0, 11), (11, 21), (21, 31), (31, 39), (39, NS))
+SLOTS_STEP = 8
 HALVES = 2
 HALF = NSPEC // HALVES
 KS = 2
@@ -79,19 +79,14 @@
 
     right, left, across, sibling = name(1, 0), name(3, 0), name(0, 1), name(0, 0, 1)
 
-    def load(n, width=STEP):
-        lanes = pl.ds(pl.multiple_of(n * (STEP * FINE), 128), width * FINE)
+    def load(n):
+        lanes = pl.ds(CHUNKS[n][0] * FINE, (CHUNKS[n][1] - CHUNKS[n][0]) * FINE)
         return pltpu.make_async_copy(
             volts_ref.at[0, :, :, lanes], buf.at[:, :, lanes], load_sem.at[n]
         )
 
-    last = NS - (STEPS - 1) * STEP
-
-    @pl.loop(0, STEPS - 1)
-    def _(n):
+    for n in range(len(CHUNKS)):
         load(n).start()
-
-    load(STEPS - 1, last).start()
 
     barrier = pltpu.get_barrier_semaphore()
     for other in (right, left, across, sibling):
@@ -126,30 +121,34 @@
             rank = rank + (owners[other] == owners[j]).astype(jnp.int32)
         targets.append(owners[j] * CAP + rank)
 
-    @pl.loop(0, nchan * CAP)
-    def _(slot):
+    for slot in range(nchan * CAP):
         found = jnp.int32(0)
         for j in range(1, KEEP):
             found = jnp.where(targets[j] == slot, j, found)
         pick[slot] = found
 
-    def transform(n):
-        at = n * (STEP * FINE)
-        for pair in range(STEP // 2):
-            block = jnp.concatenate(
-                [
-                    buf[:, :, pl.ds(pl.multiple_of(at + (pair * 2 + u) * FINE, 128), FINE)].reshape(
-                        128, FINE
-                    )
-                    for u in range(2)
-                ],
-                0,
-            )
-            product = lax.dot_general(
-                weights[...], block, (((1,), (1,)), ((), ())), preferred_element_type=F32
-            )
-            for u in range(2):
-                partial[n * STEP + pair * 2 + u] = product[:, u * 128 : (u + 1) * 128]
+    def transform(first, width):
+        block = jnp.concatenate(
+            [
+                buf[:, :, (first + u) * FINE : (first + u + 1) * FINE].reshape(128, FINE)
+                for u in range(width)
+            ],
+            0,
+        )
+        product = lax.dot_general(
+            weights[...], block, (((1,), (1,)), ((), ())), preferred_element_type=F32
+        )
+        for u in range(width):
+            partial[first + u] = product[:, u * 128 : (u + 1) * 128]
+
+    def finish(t):
+        total = partial[t, 0:16, :]
+        for p in range(1, TAPS):
+            total = total + partial[t + p, p * 16 : (p + 1) * 16, :]
+        swapped = swap_halves(total[8:16])
+        rows[pl.ds(t % HALF, KEEP, stride=HALF), :] = total[0:8] + jnp.where(
+            lane < 64, swapped, -swapped
+        )
 
     lane = lax.broadcasted_iota(jnp.int32, (KEEP, 128), 1)
 
@@ -164,40 +163,24 @@
             device_id_type=MESH,
         )
 
+    chunk = 0
     done = 0
     for half in range(HALVES):
-        upto = ((half + 1) * HALF + TAPS - 1 + STEP - 1) // STEP
-
-        @pl.loop(done, upto)
-        def _(n):
-            @pl.when(n < STEPS - 1)
-            def _():
-                load(n).wait()
-
-            @pl.when(n == STEPS - 1)
-            def _():
-                load(STEPS - 1, last).wait()
-
-            transform(n)
-
-        done = upto
-
-        @pl.loop(0, HALF)
-        def _(t):
-            at = half * HALF + t
-            total = partial[at, 0:16, :]
-            for p in range(1, TAPS):
-                total = total + partial[at + p, p * 16 : (p + 1) * 16, :]
-            swapped = swap_halves(total[8:16])
-            rows[pl.ds(t, KEEP, stride=HALF), :] = total[0:8] + jnp.where(
-                lane < 64, swapped, -swapped
-            )
+        while done < (half + 1) * HALF:
+            load(chunk).wait()
+            lo, hi = CHUNKS[chunk]
+            chunk += 1
+            for first in range(lo, hi, 2):
+                width = min(2, hi - first)
+                transform(first, width)
+                while done + TAPS <= first + width and done < (half + 1) * HALF:
+                    finish(done)
+                    done += 1
 
         for j in range(KEEP):
             channels[j] = rows[j * HALF : (j + 1) * HALF, :].astype(BF16)
 
-        @pl.loop(0, nchan * CAP)
-        def _(slot):
+        for slot in range(nchan * CAP):
             outbox[half, slot] = channels[pick[slot]]
 
         if half == 0:
@@ -351,9 +334,9 @@
         ],
         out_specs=pl.BlockSpec(memory_space=pltpu.VMEM),
         scratch_shapes=[
-            pltpu.VMEM((2, inputs, STEPS * STEP * FINE), BF16),
+            pltpu.VMEM((2, inputs, NS * FINE), BF16),
             pltpu.VMEM((TAPS * 16, FINE), BF16),
-            pltpu.VMEM((STEPS * STEP, TAPS * 16, lanes), F32),
+            pltpu.VMEM((NS, TAPS * 16, lanes), F32),
             pltpu.VMEM((KEEP * HALF, lanes), F32),
             pltpu.VMEM((KEEP, HALF, lanes), BF16),
             pltpu.VMEM((HALVES, nchan * CAP, HALF, lanes), BF16),
@@ -361,7 +344,7 @@
             pltpu.VMEM((nchan * CAP, HALF, lanes), BF16),
             pltpu.SMEM((nchan * CAP,), jnp.int32),
             pltpu.SMEM((RCAP,), jnp.int32),
-            dma((STEPS,)),
+            dma((len(CHUNKS),)),
             dma((HALVES, nchan)),
             dma((HALVES, nchan)),
             dma((8, KCH)),
@@ -386,8 +369,7 @@
     def store(slot):
         return pltpu.make_async_copy(built.at[slot], out_ref.at[0, slot], sems.at[slot])
 
-    @pl.loop(0, RCAP)
-    def _(slot):
+    def correlate_slot(slot):
         own = series(stn, slot) * (1.0 / NSPEC)
         turned = swap_halves(own)
         turned = jnp.where(low, turned, -turned)
@@ -408,6 +390,11 @@
             built[slot, :, :, n * 64 : (n + 4) * 64] = product.astype(BF16).reshape(2, 64, 256)
         store(slot).start()
 
+    @pl.loop(0, RCAP // SLOTS_STEP)
+    def _(step):
+        for u in range(SLOTS_STEP):
+            correlate_slot(step * SLOTS_STEP + u)
+
     @pl.loop(0, RCAP)
     def _(slot):
         store(slot).wait()
@@ -431,7 +418,8 @@
 
 
 def per_device(volts, taps, survive, owner):
-    gathered = front(volts, taps, survive.T, owner.T, lax.axis_size("stn"))
+    volts, taps, survive, owner = [pltpu.with_memory_space_constraint(v, pltpu.HBM) for v in (volts, taps, survive.T, owner.T)]
+    gathered = front(volts, taps, survive, owner, lax.axis_size("stn"))
     return correlate(gathered)
 
 

time: 50.1 us -> 41.3 us (0.82)
  Pallas kernels: 47.8 us -> 41.2 us
  local copies, waits for them, and re-layouts: 2.11 us -> 0 us
    pallas_call x1, Pallas kernels: 8.88 us -> 4.05 us  [correlate(): pl.pallas_call(functools.partial(correlate_kernel, stn_count), out_shape=...]
    unnamed x6 -> x0, local copies, waits for them, and re-layouts: 2.11 us -> none
    pallas_call x1, Pallas kernels: 38.9 us -> 37.1 us  [front(): pl.pallas_call(front_kernel, out_shape=jax.ShapeDtypeStruct((HALVES, stn_...]
where the time goes in v3:
time: 41.3 us; the launch traced here: 41.2 us
  Pallas kernels  41.2 us (100%)
    pallas_call x1, Pallas kernels, front(): pl.pallas_call(front_kernel, out_shape=jax.ShapeDtypeStruct((HALVES, stn_...  37.1 us
    pallas_call x1, Pallas kernels, correlate(): pl.pallas_call(functools.partial(correlate_kernel, stn_count), out_shape=...  4.05 us

profile of v3, /device:TPU:1, one launch (start us, length us, event | category | flops | bytes accessed | tf_op | source)
XLA Modules:
  0.0 41.2 jit_solution(2462936115687401274)
XLA Ops:
  0.0 37.1 %front.1.gathered = bf16[2,16,24,16,128]{4,3,2,1,0:T(8,128)(2,1)S(1)} custom-call(s32[8,16]{1,0:T(8,128)} %bitcast.2, s32[8,16]{1,0:T(8,128)} %bitcast.3, f32[16,384]{1,0:T(8,128)} %taps_ref.1, bf16[1,2,64,18048]{3,2,1,0:T(8,128)(2,1)} %volts_ref.1), custom_call_target="tpu_custom_call" | custom-call | tf_op jit(solution)/shard_map/front/pallas_call | solution.py:326
  37.1 4.0 %correlate.1 = bf16[1,24,2,64,1024]{4,3,2,1,0:T(8,128)(2,1)} custom-call(bf16[2,16,24,16,128]{4,3,2,1,0:T(8,128)(2,1)S(1)} %front.1.gathered), custom_call_target="tpu_custom_call" | custom-call | tf_op jit(solution)/shard_map/correlate/pallas_call | solution.py:406

commit v4 on v3

--- a/solution.py
+++ b/solution.py
@@ -50,13 +50,11 @@
     return ((c * factor).astype(BF16).astype(F32), (s * factor).astype(BF16).astype(F32))
 
 
-CHUNKS = ((0, 11), (11, 21), (21, 31), (31, 39), (39, NS))
+CHUNKS = ((0, 12), (12, 23), (23, 31), (31, 39), (39, NS))
 SLOTS_STEP = 8
-HALVES = 2
-HALF = NSPEC // HALVES
-KS = 2
-PER = RCAP // KS
-KCH = HALVES * KS
+PARTS = 4
+SPAN = NSPEC // PARTS
+GROUPS = ((0, 1), (1, 2), (2, 4))
 OWN, Y0, R0, L0, R1, L1, F0, F1 = range(8)
 PLACES = {
     OWN: (0, 0), Y0: (0, 1), R0: (1, 0), L0: (3, 0), R1: (1, 1), L1: (3, 1), F0: (2, 0), F1: (2, 1)
@@ -64,11 +62,11 @@
 
 
 def front_kernel(
-    survive_ref, owner_ref, taps_ref, volts_ref, gathered,
-    buf, weights, partial, rows, channels, outbox, arrived0, arrived1, pick, source,
-    load_sem, send1, recv1, send2, recv2, sib_send, sib_recv,
+    survive_hbm, owner_hbm, taps_hbm, volts_ref, gathered,
+    survive_ref, owner_ref, taps_ref, buf, weights, partial, rows, channels, outbox, arrived0, arrived1, arrived2, pick, source,
+    small_sem, load_sem, send1, recv1, send2, recv2, sib_send, sib_recv,
 ):
-    arrived = (arrived0, arrived1)
+    arrived = (arrived0, arrived1, arrived2)
     stn = lax.axis_index("stn")
     chan = lax.axis_index("chan")
     nchan = lax.axis_size("chan")
@@ -85,6 +83,14 @@
             volts_ref.at[0, :, :, lanes], buf.at[:, :, lanes], load_sem.at[n]
         )
 
+    small = [
+        pltpu.make_async_copy(source, target, small_sem.at[n])
+        for n, (source, target) in enumerate(
+            ((survive_hbm, survive_ref), (taps_hbm, taps_ref), (owner_hbm, owner_ref))
+        )
+    ]
+    for copy in small:
+        copy.start()
     for n in range(len(CHUNKS)):
         load(n).start()
 
@@ -102,6 +108,9 @@
             device_id={"stn": stn, "chan": (chan + step) % nchan},
             device_id_type=MESH,
         )
+
+    for copy in small:
+        copy.wait()
 
     row = lax.broadcasted_iota(jnp.int32, (KEEP, FINE), 0)
     branch = lax.broadcasted_iota(jnp.int32, (KEEP, FINE), 1).astype(F32)
@@ -146,51 +155,54 @@
         for p in range(1, TAPS):
             total = total + partial[t + p, p * 16 : (p + 1) * 16, :]
         swapped = swap_halves(total[8:16])
-        rows[pl.ds(t % HALF, KEEP, stride=HALF), :] = total[0:8] + jnp.where(
+        rows[pl.ds(t % SPAN, KEEP, stride=SPAN), :] = total[0:8] + jnp.where(
             lane < 64, swapped, -swapped
         )
 
     lane = lax.broadcasted_iota(jnp.int32, (KEEP, 128), 1)
 
-    def turn(half, step):
+    def turn(group, step):
         to = (chan + step) % nchan
+        lo, hi = GROUPS[group]
         return pltpu.make_async_remote_copy(
-            src_ref=outbox.at[half, pl.ds(to * CAP, CAP)],
-            dst_ref=arrived[half].at[pl.ds(chan * CAP, CAP)],
-            send_sem=send1.at[half, step],
-            recv_sem=recv1.at[half, step],
+            src_ref=outbox.at[lo:hi, pl.ds(to * CAP, CAP)],
+            dst_ref=arrived[group].at[:, pl.ds(chan * CAP, CAP)],
+            send_sem=send1.at[group, step],
+            recv_sem=recv1.at[group, step],
             device_id={"stn": stn, "chan": to},
             device_id_type=MESH,
         )
 
     chunk = 0
     done = 0
-    for half in range(HALVES):
-        while done < (half + 1) * HALF:
-            load(chunk).wait()
-            lo, hi = CHUNKS[chunk]
-            chunk += 1
-            for first in range(lo, hi, 2):
-                width = min(2, hi - first)
-                transform(first, width)
-                while done + TAPS <= first + width and done < (half + 1) * HALF:
-                    finish(done)
-                    done += 1
-
-        for j in range(KEEP):
-            channels[j] = rows[j * HALF : (j + 1) * HALF, :].astype(BF16)
-
-        for slot in range(nchan * CAP):
-            outbox[half, slot] = channels[pick[slot]]
-
-        if half == 0:
+    for group, (lo, hi) in enumerate(GROUPS):
+        for q in range(lo, hi):
+            while done < (q + 1) * SPAN:
+                load(chunk).wait()
+                begin, end = CHUNKS[chunk]
+                chunk += 1
+                for first in range(begin, end, 2):
+                    width = min(2, end - first)
+                    transform(first, width)
+                    while done + TAPS <= first + width and done < (q + 1) * SPAN:
+                        finish(done)
+                        done += 1
+
+            for j in range(KEEP):
+                channels[j] = rows[j * SPAN : (j + 1) * SPAN, :].astype(BF16)
+            for slot in range(nchan * CAP):
+                outbox[q, slot] = channels[pick[slot]]
+
+        if group == 0:
             pl.semaphore_wait(barrier, 4 + nchan - 1)
 
         @pl.loop(0, nchan - 1)
         def _(i):
-            turn(half, nchan // 2 + ((i + 1) // 2) * (2 * (i % 2) - 1)).start()
-
-        arrived[half][pl.ds(chan * CAP, CAP)] = outbox[half, pl.ds(chan * CAP, CAP)]
+            turn(group, nchan // 2 + ((i + 1) // 2) * (2 * (i % 2) - 1)).start()
+
+        for q in range(lo, hi):
+            mine = pl.ds(chan * CAP, CAP)
+            arrived[group][q - lo, mine] = outbox[q, mine]
 
     counts = []
     count = jnp.int32(0)
@@ -210,11 +222,11 @@
 
     def part(block, k):
         dx, dy = PLACES[block]
-        return gathered.at[k // KS, name(dx, dy), pl.ds((k % KS) * PER, PER)]
-
-    def whole(block, half, dcore=0):
+        return gathered.at[k, name(dx, dy)]
+
+    def two(block, half, dcore=0):
         dx, dy = PLACES[block]
-        return gathered.at[half, name(dx, dy, dcore)]
+        return gathered.at[2 * half : 2 * half + 2, name(dx, dy, dcore)]
 
     def push(block, k, to, slot):
         copy = pltpu.make_async_remote_copy(
@@ -228,19 +240,27 @@
         copy.start()
         sends.append(copy)
 
-    def share(block, k):
-        if k % KS < KS - 1:
-            return
+    def share(block, half):
         copy = pltpu.make_async_remote_copy(
-            src_ref=whole(block, k // KS),
-            dst_ref=whole(block, k // KS),
-            send_sem=sib_send.at[block, k // KS],
-            recv_sem=sib_recv.at[block, k // KS],
+            src_ref=two(block, half),
+            dst_ref=two(block, half),
+            send_sem=sib_send.at[block, half],
+            recv_sem=sib_recv.at[block, half],
             device_id={"stn": sibling, "chan": chan},
             device_id_type=MESH,
         )
         copy.start()
         sends.append(copy)
+
+    def from_sibling(block, half):
+        pltpu.make_async_remote_copy(
+            src_ref=two(block, half, 1),
+            dst_ref=two(block, half, 1),
+            send_sem=sib_send.at[block, half],
+            recv_sem=sib_recv.at[block, half],
+            device_id={"stn": sibling, "chan": chan},
+            device_id_type=MESH,
+        ).wait_recv()
 
     def arrive(block, k):
         pltpu.make_async_remote_copy(
@@ -252,69 +272,95 @@
             device_id_type=MESH,
         ).wait_recv()
 
-    for half in range(HALVES):
-
+    def own(group):
         @pl.loop(1, nchan)
         def _(step):
-            turn(half, step).wait_recv()
-
-        @pl.loop(0, RCAP)
-        def _(r):
-            block = arrived[half][source[r]]
-            gathered[half, stn, r] = jnp.where(r < count, block, jnp.zeros_like(block))
-
-        for k in range(half * KS, (half + 1) * KS):
+            turn(group, step).wait_recv()
+
+        lo, hi = GROUPS[group]
+        for k in range(lo, hi):
+
+            @pl.loop(0, RCAP, unroll=4)
+            def _(r):
+                block = arrived[group][k - lo, source[r]]
+                gathered[k, stn, r] = jnp.where(r < count, block, jnp.zeros_like(block))
+
             push(OWN, k, right, L0)
             push(OWN, k, left, R0)
             push(OWN, k, across, Y0)
-            share(OWN, k)
+
+    def beside(k):
+        if k % 2 == 0:
+            arrive(R0, k)
+            push(R0, k, left, F0)
+            arrive(L0, k)
+        else:
+            arrive(L0, k)
+            push(L0, k, right, F0)
+            arrive(R0, k)
+
+    def pair(k):
+        arrive(Y0, k)
+        push(Y0, k, right, L1)
+        push(Y0, k, left, R1)
 
     def far(k):
         arrive(F0, k)
         push(F0, k, across, F1)
-        share(F0, k)
-
-    for k in range(KCH):
-        arrive(R0, k)
-        if k % 2 == 0:
-            push(R0, k, left, F0)
-        arrive(L0, k)
-        if k % 2 == 1:
-            push(L0, k, right, F0)
-        arrive(Y0, k)
-        push(Y0, k, right, L1)
-        push(Y0, k, left, R1)
-        for block in (R0, L0, Y0):
-            share(block, k)
-        if k >= 2:
-            far(k - 2)
-    for k in range(KCH - 2, KCH):
-        far(k)
-    for k in range(KCH):
-        arrive(R1, k)
-        share(R1, k)
-        arrive(L1, k)
-        share(L1, k)
-    for k in range(KCH):
-        arrive(F1, k)
-        share(F1, k)
-    for block in range(8):
-        for half in range(HALVES):
-            pltpu.make_async_remote_copy(
-                src_ref=whole(block, half, 1),
-                dst_ref=whole(block, half, 1),
-                send_sem=sib_send.at[block, half],
-                recv_sem=sib_recv.at[block, half],
-                device_id={"stn": sibling, "chan": chan},
-                device_id_type=MESH,
-            ).wait_recv()
-    for half in range(HALVES):
+
+    own(0)
+    own(1)
+    share(OWN, 0)
+    beside(0)
+    pair(0)
+    own(2)
+    beside(1)
+    pair(1)
+    share(OWN, 1)
+    far(0)
+    for block in (R0, L0, Y0):
+        share(block, 0)
+    beside(2)
+    beside(3)
+    pair(2)
+    pair(3)
+    far(1)
+    for group in range(len(GROUPS)):
 
         @pl.loop(1, nchan)
         def _(step):
-            turn(half, step).wait_send()
-
-    for copy in sends:
+            turn(group, step).wait_send()
+
+    share(R0, 1)
+    share(L0, 1)
+    share(Y0, 1)
+    share(F0, 0)
+    early = len(sends)
+    far(2)
+    far(3)
+    share(F0, 1)
+    for block in (R1, L1, F1):
+        arrive(block, 0)
+        arrive(block, 1)
+        share(block, 0)
+    for copy in sends[:early]:
+        copy.wait_send()
+    for half in range(2):
+        for block in (OWN, R0, L0, Y0):
+            from_sibling(block, half)
+    for block in (R1, L1):
+        arrive(block, 2)
+    arrive(R1, 3)
+    share(R1, 1)
+    arrive(L1, 3)
+    share(L1, 1)
+    arrive(F1, 2)
+    arrive(F1, 3)
+    share(F1, 1)
+    for half in range(2):
+        for block in (F0, R1, L1, F1):
+            from_sibling(block, half)
+    for copy in sends[early:]:
         copy.wait_send()
 
 
@@ -325,32 +371,30 @@
     dma = pltpu.SemaphoreType.DMA
     return pl.pallas_call(
         front_kernel,
-        out_shape=jax.ShapeDtypeStruct((HALVES, stn_count, RCAP, HALF, lanes), BF16),
-        in_specs=[
-            pl.BlockSpec(memory_space=pltpu.SMEM),
-            pl.BlockSpec(memory_space=pltpu.SMEM),
-            pl.BlockSpec(memory_space=pltpu.VMEM),
-            pl.BlockSpec(memory_space=pltpu.HBM),
-        ],
+        out_shape=jax.ShapeDtypeStruct((PARTS, stn_count, RCAP, SPAN, lanes), BF16),
+        in_specs=[pl.BlockSpec(memory_space=pltpu.HBM)] * 4,
         out_specs=pl.BlockSpec(memory_space=pltpu.VMEM),
         scratch_shapes=[
+            pltpu.SMEM(survive.shape, jnp.int32),
+            pltpu.SMEM(owner.shape, jnp.int32),
+            pltpu.VMEM(taps.shape, F32),
             pltpu.VMEM((2, inputs, NS * FINE), BF16),
             pltpu.VMEM((TAPS * 16, FINE), BF16),
             pltpu.VMEM((NS, TAPS * 16, lanes), F32),
-            pltpu.VMEM((KEEP * HALF, lanes), F32),
-            pltpu.VMEM((KEEP, HALF, lanes), BF16),
-            pltpu.VMEM((HALVES, nchan * CAP, HALF, lanes), BF16),
-            pltpu.VMEM((nchan * CAP, HALF, lanes), BF16),
-            pltpu.VMEM((nchan * CAP, HALF, lanes), BF16),
+            pltpu.VMEM((KEEP * SPAN, lanes), F32),
+            pltpu.VMEM((KEEP, SPAN, lanes), BF16),
+            pltpu.VMEM((PARTS, nchan * CAP, SPAN, lanes), BF16),
+            *[pltpu.VMEM((hi - lo, nchan * CAP, SPAN, lanes), BF16) for lo, hi in GROUPS],
             pltpu.SMEM((nchan * CAP,), jnp.int32),
             pltpu.SMEM((RCAP,), jnp.int32),
+            dma((3,)),
             dma((len(CHUNKS),)),
-            dma((HALVES, nchan)),
-            dma((HALVES, nchan)),
-            dma((8, KCH)),
-            dma((8, KCH)),
-            dma((8, HALVES)),
-            dma((8, HALVES)),
+            dma((len(GROUPS), nchan)),
+            dma((len(GROUPS), nchan)),
+            dma((8, PARTS)),
+            dma((8, PARTS)),
+            dma((8, 2)),
+            dma((8, 2)),
         ],
         compiler_params=pltpu.CompilerParams(
             collective_id=0, has_side_effects=True, vmem_limit_bytes=48 << 20
@@ -364,7 +408,7 @@
     low = lax.broadcasted_iota(jnp.int32, (NSPEC, 128), 1) < 64
 
     def series(n, slot):
-        return jnp.concatenate([gathered[h, n, slot] for h in range(HALVES)], 0).astype(F32)
+        return jnp.concatenate([gathered[k, n, slot].astype(F32) for k in range(PARTS)], 0)
 
     def store(slot):
         return pltpu.make_async_copy(built.at[slot], out_ref.at[0, slot], sems.at[slot])

time: 41.3 us -> 39.9 us (0.966)
  Pallas kernels: 41.2 us -> 39.8 us
    pallas_call x1, Pallas kernels: 37.1 us -> 35.8 us  [front(): pl.pallas_call(front_kernel, out_shape=jax.ShapeDtypeStruct((PARTS, stn_c...]
where the time goes in v4:
time: 39.9 us; the launch traced here: 39.8 us
  Pallas kernels  39.8 us (100%)
    pallas_call x1, Pallas kernels, front(): pl.pallas_call(front_kernel, out_shape=jax.ShapeDtypeStruct((PARTS, stn_c...  35.8 us
    pallas_call x1, Pallas kernels, correlate(): pl.pallas_call(functools.partial(correlate_kernel, stn_count), out_shape=...  4.07 us

profile of v4, /device:TPU:1, one launch (start us, length us, event | category | flops | bytes accessed | tf_op | source)
XLA Modules:
  0.0 39.8 jit_solution(11928972814370984194)
XLA Ops:
  0.0 35.8 %front.1.gathered = bf16[4,16,24,8,128]{4,3,2,1,0:T(8,128)(2,1)S(1)} custom-call(s32[8,16]{1,0:T(8,128)} %bitcast.2, s32[8,16]{1,0:T(8,128)} %bitcast.3, f32[16,384]{1,0:T(8,128)} %taps_hbm.1, bf16[1,2,64,18048]{3,2,1,0:T(8,128)(2,1)} %volts_ref.1), custom_call_target="tpu_custom_call" | custom-call | tf_op jit(solution)/shard_map/front/pallas_call | solution.py:372
  35.8 4.1 %correlate.1 = bf16[1,24,2,64,1024]{4,3,2,1,0:T(8,128)(2,1)} custom-call(bf16[4,16,24,8,128]{4,3,2,1,0:T(8,128)(2,1)S(1)} %front.1.gathered), custom_call_target="tpu_custom_call" | custom-call | tf_op jit(solution)/shard_map/correlate/pallas_call | solution.py:450

commit v5 on v4

--- a/solution.py
+++ b/solution.py
@@ -54,7 +54,7 @@
 SLOTS_STEP = 8
 PARTS = 4
 SPAN = NSPEC // PARTS
-GROUPS = ((0, 1), (1, 2), (2, 4))
+GROUPS = ((0, 2), (2, 4))
 OWN, Y0, R0, L0, R1, L1, F0, F1 = range(8)
 PLACES = {
     OWN: (0, 0), Y0: (0, 1), R0: (1, 0), L0: (3, 0), R1: (1, 1), L1: (3, 1), F0: (2, 0), F1: (2, 1)
@@ -63,17 +63,23 @@
 
 def front_kernel(
     survive_hbm, owner_hbm, taps_hbm, volts_ref, gathered,
-    survive_ref, owner_ref, taps_ref, buf, weights, partial, rows, channels, outbox, arrived0, arrived1, arrived2, pick, source,
+    survive_ref, owner_ref, taps_ref, buf, weights, partial, rows, channels, outbox, arrived0, arrived1, pick, source,
     small_sem, load_sem, send1, recv1, send2, recv2, sib_send, sib_recv,
 ):
-    arrived = (arrived0, arrived1, arrived2)
+    arrived = (arrived0, arrived1)
     stn = lax.axis_index("stn")
     chan = lax.axis_index("chan")
     nchan = lax.axis_size("chan")
-    x, y, core = stn // 4, (stn // 2) % 2, stn % 2
+    x, y, core = lax.div(stn, 4), lax.rem(lax.div(stn, 2), 2), lax.rem(stn, 2)
+    names = {
+        (dx, dy, dcore): lax.rem(x + dx, 4) * 4 + lax.rem(y + dy, 2) * 2 + lax.rem(core + dcore, 2)
+        for dx in range(4)
+        for dy in range(2)
+        for dcore in range(2)
+    }
 
     def name(dx, dy, dcore=0):
-        return ((x + dx) % 4) * 4 + ((y + dy) % 2) * 2 + (core + dcore) % 2
+        return names[dx, dy, dcore]
 
     right, left, across, sibling = name(1, 0), name(3, 0), name(0, 1), name(0, 0, 1)
 
@@ -162,7 +168,7 @@
     lane = lax.broadcasted_iota(jnp.int32, (KEEP, 128), 1)
 
     def turn(group, step):
-        to = (chan + step) % nchan
+        to = lax.rem(chan + step, nchan)
         lo, hi = GROUPS[group]
         return pltpu.make_async_remote_copy(
             src_ref=outbox.at[lo:hi, pl.ds(to * CAP, CAP)],
@@ -196,8 +202,7 @@
         if group == 0:
             pl.semaphore_wait(barrier, 4 + nchan - 1)
 
-        @pl.loop(0, nchan - 1)
-        def _(i):
+        for i in range(nchan - 1):
             turn(group, nchan // 2 + ((i + 1) // 2) * (2 * (i % 2) - 1)).start()
 
         for q in range(lo, hi):
@@ -309,12 +314,11 @@
         push(F0, k, across, F1)
 
     own(0)
+    share(OWN, 0)
     own(1)
-    share(OWN, 0)
     beside(0)
+    beside(1)
     pair(0)
-    own(2)
-    beside(1)
     pair(1)
     share(OWN, 1)
     far(0)

time: 39.9 us -> 40.1 us (level)
  no operation moved by 1% of the time
where the time goes in v5:
time: 40.1 us
  Pallas kernels  40.1 us (100%)
    pallas_call x1, Pallas kernels, front(): pl.pallas_call(front_kernel, out_shape=jax.ShapeDtypeStruct((PARTS, stn_c...  36 us
    pallas_call x1, Pallas kernels, correlate(): pl.pallas_call(functools.partial(correlate_kernel, stn_count), out_shape=...  4.07 us

profile of v5, /device:TPU:1, one launch (start us, length us, event | category | flops | bytes accessed | tf_op | source)
XLA Modules:
  0.0 40.1 jit_solution(5452430500018016871)
XLA Ops:
  0.0 36.0 %front.1.gathered = bf16[4,16,24,8,128]{4,3,2,1,0:T(8,128)(2,1)S(1)} custom-call(s32[8,16]{1,0:T(8,128)} %bitcast.2, s32[8,16]{1,0:T(8,128)} %bitcast.3, f32[16,384]{1,0:T(8,128)} %taps_hbm.1, bf16[1,2,64,18048]{3,2,1,0:T(8,128)(2,1)} %volts_ref.1), custom_call_target="tpu_custom_call" | custom-call | tf_op jit(solution)/shard_map/front/pallas_call | solution.py:376
  36.0 4.1 %correlate.1 = bf16[1,24,2,64,1024]{4,3,2,1,0:T(8,128)(2,1)} custom-call(bf16[4,16,24,8,128]{4,3,2,1,0:T(8,128)(2,1)S(1)} %front.1.gathered), custom_call_target="tpu_custom_call" | custom-call | tf_op jit(solution)/shard_map/correlate/pallas_call | solution.py:454

commit v6 on v4

--- a/solution.py
+++ b/solution.py
@@ -54,7 +54,7 @@
 SLOTS_STEP = 8
 PARTS = 4
 SPAN = NSPEC // PARTS
-GROUPS = ((0, 1), (1, 2), (2, 4))
+GROUPS = ((0, 1), (1, 2), (2, 3), (3, 4))
 OWN, Y0, R0, L0, R1, L1, F0, F1 = range(8)
 PLACES = {
     OWN: (0, 0), Y0: (0, 1), R0: (1, 0), L0: (3, 0), R1: (1, 1), L1: (3, 1), F0: (2, 0), F1: (2, 1)
@@ -63,10 +63,10 @@
 
 def front_kernel(
     survive_hbm, owner_hbm, taps_hbm, volts_ref, gathered,
-    survive_ref, owner_ref, taps_ref, buf, weights, partial, rows, channels, outbox, arrived0, arrived1, arrived2, pick, source,
+    survive_ref, owner_ref, taps_ref, buf, weights, partial, rows, channels, outbox, arrived0, arrived1, arrived2, arrived3, pick, source,
     small_sem, load_sem, send1, recv1, send2, recv2, sib_send, sib_recv,
 ):
-    arrived = (arrived0, arrived1, arrived2)
+    arrived = (arrived0, arrived1, arrived2, arrived3)
     stn = lax.axis_index("stn")
     chan = lax.axis_index("chan")
     nchan = lax.axis_size("chan")
@@ -314,6 +314,7 @@
     beside(0)
     pair(0)
     own(2)
+    own(3)
     beside(1)
     pair(1)
     share(OWN, 1)
@@ -418,20 +419,17 @@
         turned = swap_halves(own)
         turned = jnp.where(low, turned, -turned)
         left = jnp.concatenate([own, turned], 0).astype(BF16)
-        for n in range(0, stn_count, 4):
-            columns = []
-            for m in range(n, n + 4, 2):
-                first, second = series(m, slot), series(m + 1, slot)
-                real = jnp.where(low, first, swap_halves(second))
-                imag = jnp.where(low, swap_halves(first), second)
-                columns.append(jnp.concatenate([real, imag], 0).astype(BF16))
+        for n in range(0, stn_count, 2):
+            first, second = series(n, slot), series(n + 1, slot)
+            real = jnp.where(low, first, swap_halves(second))
+            imag = jnp.where(low, swap_halves(first), second)
             product = lax.dot_general(
                 left,
-                jnp.concatenate(columns, 1),
+                jnp.concatenate([real, imag], 0).astype(BF16),
                 (((0,), (0,)), ((), ())),
                 preferred_element_type=F32,
             )
-            built[slot, :, :, n * 64 : (n + 4) * 64] = product.astype(BF16).reshape(2, 64, 256)
+            built[slot, :, :, n * 64 : (n + 2) * 64] = product.astype(BF16).reshape(2, 64, 128)
         store(slot).start()
 
     @pl.loop(0, RCAP // SLOTS_STEP)

time: 39.9 us -> 39.9 us (level)
  no operation moved by 1% of the time
where the time goes in v6:
time: 39.9 us; the launch traced here: 39.8 us
  Pallas kernels  39.8 us (100%)
    pallas_call x1, Pallas kernels, front(): pl.pallas_call(front_kernel, out_shape=jax.ShapeDtypeStruct((PARTS, stn_c...  36.1 us
    pallas_call x1, Pallas kernels, correlate(): pl.pallas_call(functools.partial(correlate_kernel, stn_count), out_shape=...  3.75 us

profile of v6, /device:TPU:1, one launch (start us, length us, event | category | flops | bytes accessed | tf_op | source)
XLA Modules:
  0.0 39.8 jit_solution(15617013454007314550)
XLA Ops:
  0.0 36.1 %front.1.gathered = bf16[4,16,24,8,128]{4,3,2,1,0:T(8,128)(2,1)S(1)} custom-call(s32[8,16]{1,0:T(8,128)} %bitcast.2, s32[8,16]{1,0:T(8,128)} %bitcast.3, f32[16,384]{1,0:T(8,128)} %taps_hbm.1, bf16[1,2,64,18048]{3,2,1,0:T(8,128)(2,1)} %volts_ref.1), custom_call_target="tpu_custom_call" | custom-call | tf_op jit(solution)/shard_map/front/pallas_call | solution.py:373
  36.1 3.8 %correlate.1 = bf16[1,24,2,64,1024]{4,3,2,1,0:T(8,128)(2,1)} custom-call(bf16[4,16,24,8,128]{4,3,2,1,0:T(8,128)(2,1)S(1)} %front.1.gathered), custom_call_target="tpu_custom_call" | custom-call | tf_op jit(solution)/shard_map/correlate/pallas_call | solution.py:448

commit v7 on v6

--- a/solution.py
+++ b/solution.py
@@ -54,7 +54,7 @@
 SLOTS_STEP = 8
 PARTS = 4
 SPAN = NSPEC // PARTS
-GROUPS = ((0, 1), (1, 2), (2, 3), (3, 4))
+GROUPS = ((0, 1), (1, 2), (2, 4))
 OWN, Y0, R0, L0, R1, L1, F0, F1 = range(8)
 PLACES = {
     OWN: (0, 0), Y0: (0, 1), R0: (1, 0), L0: (3, 0), R1: (1, 1), L1: (3, 1), F0: (2, 0), F1: (2, 1)
@@ -63,10 +63,10 @@
 
 def front_kernel(
     survive_hbm, owner_hbm, taps_hbm, volts_ref, gathered,
-    survive_ref, owner_ref, taps_ref, buf, weights, partial, rows, channels, outbox, arrived0, arrived1, arrived2, arrived3, pick, source,
+    survive_ref, owner_ref, taps_ref, buf, weights, partial, rows, channels, outbox, arrived0, arrived1, arrived2, pick, source,
     small_sem, load_sem, send1, recv1, send2, recv2, sib_send, sib_recv,
 ):
-    arrived = (arrived0, arrived1, arrived2, arrived3)
+    arrived = (arrived0, arrived1, arrived2)
     stn = lax.axis_index("stn")
     chan = lax.axis_index("chan")
     nchan = lax.axis_size("chan")
@@ -314,7 +314,6 @@
     beside(0)
     pair(0)
     own(2)
-    own(3)
     beside(1)
     pair(1)
     share(OWN, 1)

time: 39.9 us -> 39.6 us (level)
  no operation moved by 1% of the time
where the time goes in v7:
time: 39.6 us; the launch traced here: 39.5 us
  Pallas kernels  39.5 us (100%)
    pallas_call x1, Pallas kernels, front(): pl.pallas_call(front_kernel, out_shape=jax.ShapeDtypeStruct((PARTS, stn_c...  35.8 us
    pallas_call x1, Pallas kernels, correlate(): pl.pallas_call(functools.partial(correlate_kernel, stn_count), out_shape=...  3.75 us

profile of v7, /device:TPU:1, one launch (start us, length us, event | category | flops | bytes accessed | tf_op | source)
XLA Modules:
  0.0 39.5 jit_solution(17847503951821095690)
XLA Ops:
  0.0 35.8 %front.1.gathered = bf16[4,16,24,8,128]{4,3,2,1,0:T(8,128)(2,1)S(1)} custom-call(s32[8,16]{1,0:T(8,128)} %bitcast.2, s32[8,16]{1,0:T(8,128)} %bitcast.3, f32[16,384]{1,0:T(8,128)} %taps_hbm.1, bf16[1,2,64,18048]{3,2,1,0:T(8,128)(2,1)} %volts_ref.1), custom_call_target="tpu_custom_call" | custom-call | tf_op jit(solution)/shard_map/front/pallas_call | solution.py:372
  35.8 3.8 %correlate.1 = bf16[1,24,2,64,1024]{4,3,2,1,0:T(8,128)(2,1)} custom-call(bf16[4,16,24,8,128]{4,3,2,1,0:T(8,128)(2,1)S(1)} %front.1.gathered), custom_call_target="tpu_custom_call" | custom-call | tf_op jit(solution)/shard_map/correlate/pallas_call | solution.py:447
